TPU v7x, 128 devices: a whole 4x4x4 slice. The times are simulated.
128 devices in a mesh: req: 4 (over y), hid: 32 (over x, z, core).
Axes of the slice: x: 4, y: 4, z: 4, core: 2. Of those that a mesh axis runs over, the one named last changes fastest.
Arguments:
- tokens: bfloat16 [4096, 7168], P(('req', 'hid')), may hold values from -90 to 90
- gain_in: float32 [7168], replicated, may hold values from 0.25 to 1.75
- w_qkv: bfloat16 [7168, 3, 7168], P(None, None, 'hid'), may hold values from -0.0625 to 0.0625
- adapt_down: bfloat16 [7168, 128], replicated, may hold values from -0.0625 to 0.0625
- adapt_up: bfloat16 [128, 7168], P(None, 'hid'), may hold values from -0.5 to 0.5
- w_out: bfloat16 [7168, 3584], P('hid'), may hold values from -0.0625 to 0.0625
- gain_ff: float32 [3584], replicated, may hold values from 0.25 to 1.75
- w_gate_up: bfloat16 [3584, 2, 14336], P(None, None, 'hid'), may hold values from -0.09375 to 0.09375
- w_down: bfloat16 [14336, 3584], P('hid'), may hold values from -0.046875 to 0.046875
- prefix_cache: bfloat16 [4, 2048, 2, 7168], P('req', 'hid'), may hold values from -330 to 330
- prefix_owner: int32 [3], replicated, may hold values from 0 to 3, as said below
- group_prefix: int32 [4], replicated, may hold values from 0 to 2, as said below
- lengths: int32 [4, 6], P('req'), may hold values from 1 to 512, 1024 in all within a row
Outputs:
- attn_out: bfloat16 [4096, 3584], P(('req', 'hid'))
- block_out: bfloat16 [4096, 3584], P(('req', 'hid'))
Inputs may be any that keep to these rules, and one draw needn't show every extreme that they name: `prefix_owner`: the 3 prefixes have different owners. `group_prefix`: every prefix is extended by at least one group. Each group's 6 lengths sum to 1024, and the longest of each group is exactly 512.
All inputs are finite; a program needn't handle non-finite values.
Results may differ from a plain program's by a relative error of at most 0.035.
Values may be sent and summed in bfloat16 or wider, within the bound.
A program may use at most 128 MiB of HBM per device.

v0:
```python
import jax
import jax.numpy as jnp
from jax import lax
from jax.sharding import PartitionSpec as P

HD = 224


EPS = 1e-05


def rms_scale(matrix, gain_vec):
    return matrix * lax.rsqrt(jnp.mean(matrix * matrix, axis=-1, keepdims=True) + EPS) * gain_vec


def prefix_part(queries, kv_block):
    span_len = kv_block.shape[0]
    head_count = queries.shape[1]
    head_size = queries.shape[2]
    cached_k = kv_block[:, 0].reshape(span_len, head_count, head_size)
    cached_v = kv_block[:, 1].reshape(span_len, head_count, head_size)
    scores = jnp.einsum(
        "thd,phd->htp", queries, cached_k, preferred_element_type=jnp.float32
    ) * head_size ** (-0.5)
    row_max = jnp.max(scores, axis=-1)
    expos = jnp.exp(scores - row_max[..., None])
    row_sum = jnp.sum(expos, axis=-1)
    weighted = jnp.einsum(
        "htp,phd->htd", expos.astype(jnp.bfloat16), cached_v, preferred_element_type=jnp.float32
    )
    return (row_max, row_sum, weighted)


def suffix_part(queries, suffix_keys, suffix_vals, allowed):
    head_size = queries.shape[2]
    scores = jnp.einsum(
        "thd,shd->hts", queries, suffix_keys, preferred_element_type=jnp.float32
    ) * head_size ** (-0.5)
    scores = jnp.where(allowed[None], scores, -jnp.inf)
    row_max = jnp.max(scores, axis=-1)
    expos = jnp.exp(scores - row_max[..., None])
    row_sum = jnp.sum(expos, axis=-1)
    weighted = jnp.einsum(
        "hts,shd->htd", expos.astype(jnp.bfloat16), suffix_vals, preferred_element_type=jnp.float32
    )
    return (row_max, row_sum, weighted)


def combine(first_part, second_part):
    joint_max = jnp.maximum(first_part[0], second_part[0])
    first_factor = jnp.exp(first_part[0] - joint_max)
    second_factor = jnp.exp(second_part[0] - joint_max)
    joint_sum = first_part[1] * first_factor + second_part[1] * second_factor
    joint_acc = first_part[2] * first_factor[..., None] + second_part[2] * second_factor[..., None]
    return (joint_max, joint_sum, joint_acc)


def per_device(
    tokens,
    gain_in,
    w_qkv,
    adapt_down,
    adapt_up,
    w_out,
    gain_ff,
    w_gate_up,
    w_down,
    prefix_cache,
    prefix_owner,
    group_prefix,
    lengths,
):
    tok_dev = tokens.shape[0]
    width_in = tokens.shape[1]
    head_cols = w_qkv.shape[2]
    head_count = head_cols // HD
    model_width = w_out.shape[1]
    normed = rms_scale(tokens.astype(jnp.float32), gain_in).astype(jnp.bfloat16)
    latent = jnp.dot(normed, adapt_down, preferred_element_type=jnp.float32).astype(jnp.bfloat16)
    row_block = jnp.concatenate([normed, latent], axis=1)
    joint_weight = w_qkv.reshape(width_in, 3 * head_cols)
    shard_rows = lax.all_gather(row_block, "hid", axis=0, tiled=True)
    joint = jnp.dot(shard_rows[:, :width_in], joint_weight, preferred_element_type=jnp.float32)
    query_part = joint[:, :head_cols] + jnp.dot(
        shard_rows[:, width_in:], adapt_up, preferred_element_type=jnp.float32
    )
    projected = jnp.concatenate([query_part, joint[:, head_cols:]], axis=1).astype(jnp.bfloat16)
    tok_grp = projected.shape[0]
    queries = projected[:, :head_cols].reshape(tok_grp, head_count, HD)
    suffix_keys = projected[:, head_cols : 2 * head_cols].reshape(tok_grp, head_count, HD)
    suffix_vals = projected[:, 2 * head_cols :].reshape(tok_grp, head_count, HD)
    request_ends = jnp.cumsum(lengths[0])
    position = jnp.arange(tok_grp, dtype=jnp.int32)
    request = jnp.sum((position[:, None] >= request_ends[None, :]).astype(jnp.int32), axis=1)
    allowed = jnp.logical_and(
        request[:, None] == request[None, :], position[None, :] <= position[:, None]
    )
    partial_value = suffix_part(queries, suffix_keys, suffix_vals, allowed)
    group_index = lax.axis_index("req")
    target = prefix_owner[group_prefix[group_index]]
    heads_cache = lax.all_to_all(prefix_cache[0], "hid", split_axis=2, concat_axis=0, tiled=True)
    span_len = heads_cache.shape[0]
    shard_rows = lax.all_gather(heads_cache, "req", axis=0, tiled=True)
    slot_count = shard_rows.shape[0] // span_len
    inside = jnp.logical_and(target >= 0, target < slot_count)
    chosen = lax.dynamic_slice_in_dim(
        shard_rows, jnp.clip(target, 0, slot_count - 1) * span_len, span_len, 0
    )
    partial_value = lax.cond(
        inside,
        lambda kept: combine(kept, prefix_part(queries, chosen)),
        lambda kept: kept,
        partial_value,
    )
    heads_out = (partial_value[2] / partial_value[1][..., None]).astype(jnp.bfloat16)
    out_weight = w_out.reshape(head_count, HD, model_width)
    projected_out = jnp.einsum(
        "htd,hdm->tm", heads_out, out_weight, preferred_element_type=jnp.float32
    )
    summed = lax.psum(projected_out.astype(jnp.bfloat16), "hid").astype(jnp.float32)
    hid_index = lax.axis_index("hid")
    attn_out = lax.dynamic_slice_in_dim(summed, hid_index * tok_dev, tok_dev, 0).astype(
        jnp.bfloat16
    )
    ff_in = rms_scale(summed, gain_ff).astype(jnp.bfloat16)
    unit_count = w_gate_up.shape[2]
    gate_up = jnp.dot(
        ff_in, w_gate_up.reshape(model_width, 2 * unit_count), preferred_element_type=jnp.float32
    )
    hidden = (jax.nn.silu(gate_up[:, :unit_count]) * gate_up[:, unit_count:]).astype(jnp.bfloat16)
    block_out = lax.psum_scatter(
        jnp.dot(hidden, w_down, preferred_element_type=jnp.float32).astype(jnp.bfloat16),
        "hid",
        scatter_dimension=0,
        tiled=True,
    )
    return (attn_out, block_out)


def solution(mesh):
    placed = (
        P(("req", "hid"), None),
        P(),
        P(None, None, "hid"),
        P(),
        P(None, "hid"),
        P("hid", None),
        P(),
        P(None, None, "hid"),
        P("hid", None),
        P("req", "hid", None, None),
        P(),
        P(),
        P("req", None),
    )
    return jax.shard_map(
        per_device,
        mesh=mesh,
        in_specs=placed,
        out_specs=(P(("req", "hid"), None), P(("req", "hid"), None)),
        check_vma=False,
    )
```

profile of v0, /device:TPU:1, one launch (start us, length us, event | category | flops | bytes accessed | tf_op | source)
XLA Modules:
  0.0 455.0 jit_solution(912835221307412314)
XLA Ops:
  7.2 0.0 copy-start
  7.2 0.0 all-gather.3.cloned.1.call-start
  7.2 1.4 fusion.38
  8.6 1.2 fusion.40
  9.8 1.9 convolution_convert_fusion.2
  11.7 0.8 pad_maximum_fusion
  12.5 0.0 all-gather.3.cloned.1.call-update
  12.6 0.0 all-gather.5.cloned.1.call-start
  12.6 10.1 %copy.30 = bf16[1,64,2,7168]{1,2,3,0:T(2,128)(2,1)} copy(bf16[1,64,2,7168]{3,2,1,0:T(2,128)(2,1)} %param.24) | data formatting | bytes 3670016 | tf_op args[9]
  22.7 7.1 %bitcast_bitcast_fusion = bf16[7168,2,64]{2,1,0:T(2,128)(2,1)} fusion(bf16[1,64,2,7168]{1,2,3,0:T(2,128)(2,1)} %copy.30), kind=kLoop, calls=%fused_computation.66 | loop fusion | bytes 3670016
  29.9 8.8 %reshape.147 = bf16[32,2,14336]{2,1,0:T(2,128)(2,1)} reshape(bf16[7168,2,64]{2,1,0:T(2,128)(2,1)} %bitcast_bitcast_fusion) | data formatting | bytes 3670016
  38.7 53.5 %all_to_all.18 = bf16[32,2,14336]{2,1,0:T(2,128)(2,1)} all-to-all(bf16[32,2,14336]{2,1,0:T(2,128)(2,1)} %reshape.147), channel_id=1, replica_groups=mesh['req'=4,'hid'=32] {'hid'}, dimensions={0} | all-to-all | bytes 3670016 | tf_op jit(solution)/shard_map/all_to_all | solution.py:101
  92.2 8.8 %reshape.148 = bf16[7168,2,64]{2,1,0:T(2,128)(2,1)} reshape(bf16[32,2,14336]{2,1,0:T(2,128)(2,1)} %all_to_all.18) | data formatting | bytes 3670016
  100.9 0.0 copy-start.6
  100.9 0.0 copy-start.7
  100.9 0.0 copy-start.8
  100.9 8.1 %copy.31 = bf16[64,2,32,224]{3,0,2,1:T(8,128)(2,1)} copy(bf16[64,2,32,224]{0,1,3,2:T(2,128)(2,1)} %bitcast.45) | data formatting | bytes 3670016 | tf_op jit(solution)/shard_map/all_to_all | solution.py:101
  109.1 0.0 all-gather.5.cloned.1.call-update
  109.1 0.0 all-reduce.2.cloned.1.call-start
  109.2 0.0 copy-done.6
  109.2 0.6 dynamic_slice.17
  111.7 0.0 copy-done.7
  111.7 0.6 dynamic_slice.18
  113.6 0.0 copy-done.8
  113.6 0.2 reduce-window.8
  113.8 0.1 convert_reduce_fusion
  113.9 0.0 all-gather.3.cloned.1.call-done
  113.9 0.0 copy-start.4
  113.9 15.7 %fusion.50 = (bf16[1024,672]{0,1:T(8,128)(2,1)S(1)}, f32[1024,672]{0,1:T(8,128)S(1)}) fusion(bf16[7168,672]{0,1:T(8,128)(2,1)} %bitcast.53, bf16[1024,7296]{1,0:T(8,128)(2,1)} %all-gather.3.cloned.1.call-done), kind=kOutput, calls=%fused_computation.64 | convolution fusion | flops 9865691136 | bytes 28442624 | tf_op jit(solution)/shard_map/dot_general | solution.py:83
  129.6 0.0 copy-done.4
  129.6 1.2 fusion.37
  130.9 0.0 copy-start.3
  130.9 1.1 fusion.51
  132.0 0.0 copy-done.3
  132.0 0.6 fusion.29
  132.6 1.8 fusion.34
  134.4 56.7 %all-gather.5.cloned.1.call-done = bf16[8192,2,224]{2,0,1:T(8,128)(2,1)} async-done(((bf16[2048,2,224]{2,0,1:T(8,128)(2,1)}), bf16[8192,2,224]{2,0,1:T(8,128)(2,1)}) %all-gather.5.cloned.1.call-update) | async-done | bytes 7340048 | tf_op jit(solution)/shard_map/all_gather | solution.py:103
  191.0 24.1 %conditional.1 = ((f32[1,1024]{1,0:T(1,128)S(1)}, f32[1,1024,224]{1,2,0:T(8,128)})) conditional(s32[]{:T(128)} %convert_element_type.48, (f32[1,1024]{1,0:T(1,128)S(1)}, f32[1,1024,224]{1,2,0:T(8,128)}) %tuple.50, (s32[]{:T(128)}, bf16[8192,2,224]{2,0,1:T(8,128)(2,1)}, bf16[1024,224]{0,1:T(8,128)(2,1)}, f32[1024]{0:T(1024)S(1)}, ...), branch_computations={%region_5.6_spmd, %region_6.9_spmd} | conditional | flops 1896517632 | bytes 77594776 | solution.py:109
  191.0 11.0 %copy.32 = bf16[8192,2,224]{0,2,1:T(8,128)(2,1)} copy(bf16[8192,2,224]{2,0,1:T(8,128)(2,1)} %get-tuple-element.113) | data formatting | bytes 14680064 | tf_op jit(solution)/shard_map
  202.7 2.6 multiply_reduce_fusion
  205.3 0.0 copy-start.1
  205.3 1.4 fusion.1
  206.8 1.9 copy-done.1
  208.7 6.5 %fusion.12 = f32[1,1024,224]{1,2,0:T(8,128)} fusion(f32[2048,1024]{1,0:T(8,128)} %copy-done.1, f32[1024]{0:T(1024)S(1)} %get-tuple-element.121, bf16[8192,2,224]{0,2,1:T(8,128)(2,1)} %copy.32, s32[]{:T(128)S(6)} %select_n.15, s32[]{:T(128)S(6)} %add.67, f32[1,1024,224]{1,2,0:T(8,128)} %get-tuple-element.75, f32[1024]{0:T(1024)S(1)} %get-tuple-element.119, ...), kind=kOutput, calls=%fused_computation.9 | convolution fusion | flops 946503680 | bytes 11153416 | tf_op jit(solution)/shard_map/cond/branch_1_fun/htp,phd->htd/dot_general | solution.py:28
  215.2 6.8 %convolution_convert_fusion.1 = bf16[1024,3584]{1,0:T(8,128)(2,1)} fusion(bf16[224,3584]{1,0:T(8,128)(2,1)} %param.20, f32[1,1024,224]{1,2,0:T(8,128)} %get-tuple-element.80, f32[1024]{0:T(1024)S(1)} %bitcast.49), kind=kOutput, calls=%fused_computation.26 | convolution fusion | flops 1648295936 | bytes 9867264 | tf_op jit(solution)/shard_map/htd,hdm->tm/dot_general | solution.py:117
  222.0 0.0 copy-start.5
  222.0 0.0 all-reduce.2.cloned.1.call-update
  222.0 0.3 reduce-scatter.2.cloned.1.call-start
  222.3 119.0 %all-reduce.2.cloned.1.call-done = bf16[1024,3584]{1,0:T(8,128)(2,1)} async-done(((bf16[1024,3584]{1,0:T(8,128)(2,1)}), bf16[1024,3584]{1,0:T(8,128)(2,1)}) %all-reduce.2.cloned.1.call-update) | async-done | bytes 7340048 | tf_op jit(solution)/shard_map/psum | solution.py:120
  341.3 0.0 copy-start.2
  341.3 4.7 %multiply_reduce_fusion.1 = f32[1024]{0:T(1024)S(1)} fusion(bf16[1024,3584]{1,0:T(8,128)(2,1)} %all-reduce.2.cloned.1.call-done), kind=kLoop, calls=%fused_computation.24 | loop fusion | flops 11009024 | bytes 7344128 | tf_op jit(solution)/shard_map/reduce_sum | solution.py:13
  346.0 0.0 copy-done.5
  346.0 0.4 copy-done.2
  346.4 9.1 %fusion.23 = f32[1024,896]{0,1:T(8,128)S(1)} fusion(bf16[3584,896]{0,1:T(8,128)(2,1)} %bitcast.54, f32[3584]{0:T(1024)S(1)} %copy-done.5, f32[1024]{0:T(1024)S(1)} %add_rsqrt_fusion, bf16[1024,3584]{1,0:T(8,128)(2,1)S(1)} %copy-done.2), kind=kOutput, calls=%fused_computation.27 | convolution fusion | flops 6591348736 | bytes 17451008 | tf_op jit(solution)/shard_map/dot_general | solution.py:127
  355.5 0.0 copy-done
  355.6 6.2 %convolution_convert_fusion = bf16[1024,3584]{1,0:T(8,128)(2,1)} fusion(bf16[448,3584]{1,0:T(8,128)(2,1)S(1)} %copy-done, f32[1024,896]{0,1:T(8,128)S(1)} %fusion.23), kind=kOutput, calls=%fused_computation.25 | convolution fusion | flops 3294756864 | bytes 14221312 | tf_op jit(solution)/shard_map/dot_general | solution.py:132
  361.8 0.0 reduce-scatter.2.cloned.1.call-update
  361.8 1.6 dynamic-slice_convert_fusion
  363.5 85.0 %reduce-scatter.2.cloned.1.call-done = bf16[32,3584]{1,0:T(8,128)(2,1)} async-done(((bf16[1024,3584]{1,0:T(8,128)(2,1)}), bf16[32,3584]{1,0:T(8,128)(2,1)}) %reduce-scatter.2.cloned.1.call-update) | async-done | bytes 229392 | tf_op jit(solution)/shard_map/reduce_scatter | solution.py:131
  (4 shorter events, 0.0 us)
Async XLA Ops:
  7.2 348.4 %copy-start = (bf16[448,3584]{1,0:T(8,128)(2,1)S(1)}, bf16[448,3584]{1,0:T(8,128)(2,1)}, u32[]{:S(2)}) copy-start(bf16[448,3584]{1,0:T(8,128)(2,1)} %param.23) | copy-start | bytes 9633796
  7.2 106.7 %all-gather.3.cloned.1.call-start = ((), (), s32[]{:S(2)}) async-start(), calls=%async_computation.2 | async-start | bytes 15409152 | tf_op jit(solution)/shard_map/all_gather | solution.py:82
  12.6 178.5 %all-gather.5.cloned.1.call-start = ((), (), s32[]{:S(2)}) async-start(), calls=%async_computation.3 | async-start | bytes 10485760 | tf_op jit(solution)/shard_map/all_gather | solution.py:103
  100.9 8.2 %copy-start.6 = (s32[4]{0:T(128)S(1)}, s32[4]{0:T(128)}, u32[]{:S(2)}) copy-start(s32[4]{0:T(128)} %param.26) | copy-start | bytes 52
  100.9 10.8 %copy-start.7 = (s32[3]{0:T(128)S(1)}, s32[3]{0:T(128)}, u32[]{:S(2)}) copy-start(s32[3]{0:T(128)} %param.25) | copy-start | bytes 40
  100.9 12.7 %copy-start.8 = (s32[1,6]{1,0:T(1,128)S(1)}, s32[1,6]{1,0:T(1,128)}, u32[]{:S(2)}) copy-start(s32[1,6]{1,0:T(1,128)} %param.27) | copy-start | bytes 76
  109.1 232.2 %all-reduce.2.cloned.1.call-start = ((), (), s32[]{:S(2)}) async-start(), calls=%async_computation.4 | async-start | bytes 14680064 | tf_op jit(solution)/shard_map/psum | solution.py:120
  113.9 15.7 %copy-start.4 = (bf16[128,224]{0,1:T(8,128)(2,1)S(1)}, bf16[128,224]{0,1:T(8,128)(2,1)}, u32[]{:S(2)}) copy-start(bf16[128,224]{0,1:T(8,128)(2,1)} %param.19) | copy-start | bytes 172036
  130.9 1.1 copy-start.3
  205.3 3.3 copy-start.1
  222.0 124.0 %copy-start.5 = (f32[3584]{0:T(1024)S(1)}, f32[3584]{0:T(1024)}, u32[]{:S(2)}) copy-start(f32[3584]{0:T(1024)} %param.21) | copy-start | bytes 43012
  222.0 226.4 %reduce-scatter.2.cloned.1.call-start = ((), (), s32[]{:S(2)}) async-start(), calls=%async_computation.5 | async-start | bytes 7569408 | tf_op jit(solution)/shard_map/reduce_scatter | solution.py:131
  341.3 5.2 %copy-start.2 = (bf16[1024,3584]{1,0:T(8,128)(2,1)S(1)}, bf16[1024,3584]{1,0:T(8,128)(2,1)}, u32[]{:S(2)}) copy-start(bf16[1024,3584]{1,0:T(8,128)(2,1)} %all-reduce.2.cloned.1.call-done) | copy-start | bytes 22020100
Sparse Core Ops, SparseCore 0:
  12.7 91.2 all-gather.2
  109.2 81.7 all-gather.4
  222.2 119.0 all-reduce.1
  361.9 86.5 reduce-scatter.1
where the time goes:
time: 457 us; the launch traced here: 455 us
  waiting for transfers between devices  261 us (57%)
  local copies, waits for them, and re-layouts  59.2 us (13%)
  blocking collectives  53.5 us (12%)
  matrix products  52.9 us (12%)
  between operations  17.2 us (4%)
  other arithmetic  10.5 us (2%)
    psum x1, waiting for transfers between devices, per_device(): lax.psum(projected_out.astype(jnp.bfloat16), 'hid').astype(jnp.float32)  119 us
    reduce_scatter x1, waiting for transfers between devices, per_device(): lax.psum_scatter(jnp.dot(hidden, w_down, preferred_element_type=jnp.float...  85 us
    all_gather x1, waiting for transfers between devices, per_device(): shard_rows = lax.all_gather(heads_cache, 'req', axis=0, tiled=True)  56.7 us
    all_to_all x1, blocking collectives, per_device(): lax.all_to_all(prefix_cache[0], 'hid', split_axis=2, concat_axis=0, tiled...  53.5 us
    unnamed x20, local copies, waits for them, and re-layouts  35.3 us
    dot_general x1, matrix products, per_device(): jnp.dot(shard_rows[:, :width_in], joint_weight, preferred_element_type=jn...  15.7 us
    another operation x1, local copies, waits for them, and re-layouts  11 us
  transfers between devices with their start and end apart: 4, of which 3 were waited for; matrix products, arithmetic and copies ran while one was open for 15% of the time, Pallas kernels for 0%

commit v1 on v0

--- a/solution.py
+++ b/solution.py
@@ -1,6 +1,8 @@
 import jax
 import jax.numpy as jnp
 from jax import lax
+from jax.experimental import pallas as pl
+from jax.experimental.pallas import tpu as pltpu
 from jax.sharding import PartitionSpec as P
 
 HD = 224
@@ -53,6 +55,344 @@
     joint_sum = first_part[1] * first_factor + second_part[1] * second_factor
     joint_acc = first_part[2] * first_factor[..., None] + second_part[2] * second_factor[..., None]
     return (joint_max, joint_sum, joint_acc)
+
+
+MESH = pl.DeviceIdType.MESH
+NX, NZ = 4, 4
+
+
+def place():
+    hid = lax.axis_index("hid")
+    return hid // 8, (hid // 2) % 4, hid % 2
+
+
+def moved(da, db, core_flip=0):
+    x, z, c = place()
+    xn = (x + 4 + (1 - c) * db + c * da) % 4
+    zn = (z + 4 + (1 - c) * da + c * db) % 4
+    cn = c + core_flip * (1 - 2 * c)
+    return xn * 8 + zn * 2 + cn
+
+
+def remote(src, dst, send, recv, hid):
+    return pltpu.make_async_remote_copy(
+        src_ref=src, dst_ref=dst, send_sem=send, recv_sem=recv,
+        device_id={"hid": hid}, device_id_type=MESH,
+    )
+
+
+def greet(peers):
+    barrier = pltpu.get_barrier_semaphore()
+    for peer in peers:
+        pl.semaphore_signal(barrier, inc=1, device_id=peer, device_id_type=MESH)
+    pl.semaphore_wait(barrier, len(peers))
+
+
+class Mail:
+    def __init__(self, send_sems, recv_sems):
+        self.send_sems, self.recv_sems, self.sent = send_sems, recv_sems, []
+
+    def send(self, role, src, dst, hid):
+        copy = remote(src, dst, self.send_sems.at[role], self.recv_sems.at[role], hid)
+        copy.start()
+        self.sent.append(copy)
+
+    def await_recv(self, role, dst, hid):
+        remote(dst, dst, self.send_sems.at[role], self.recv_sems.at[role], hid).wait_recv()
+
+    def drain(self):
+        for copy in self.sent:
+            copy.wait_send()
+
+
+GATHER_ROLES = 36
+
+
+def gather_rows(mail, base, buf, rows, on_pair=None):
+    half = rows // 2
+    x, z, c = place()
+
+    def blk(hid, part=None):
+        start = pl.multiple_of(hid * rows, rows)
+        if part is None:
+            return buf.at[pl.ds(start, rows)]
+        return buf.at[pl.ds(start + part * half, half)]
+
+    offs = (0, -1, 1, 2)
+    a_plus, a_minus = moved(1, 0), moved(-1, 0)
+    b_plus, b_minus = moved(0, 1), moved(0, -1)
+    partner = moved(0, 0, 1)
+
+    def role2(i, k):
+        return base + 4 + 4 * i + k
+
+    def to_partner(ia, ib):
+        owner = moved(offs[ia], offs[ib])
+        mail.send(base + 20 + ia * 4 + ib, blk(owner), blk(owner), partner)
+
+    def line_out(i):
+        owner = moved(0, offs[i])
+        mail.send(role2(i, 0), blk(owner), blk(owner), a_plus)
+        mail.send(role2(i, 1), blk(owner), blk(owner), a_minus)
+
+    def line_relay(i):
+        low, high = moved(-1, offs[i]), moved(1, offs[i])
+        mail.await_recv(role2(i, 0), blk(low), a_minus)
+        mail.send(role2(i, 2), blk(low, 0), blk(low, 0), a_plus)
+        mail.await_recv(role2(i, 1), blk(high), a_plus)
+        mail.send(role2(i, 3), blk(high, 1), blk(high, 1), a_minus)
+        to_partner(1, i)
+        to_partner(2, i)
+
+    def line_far(i):
+        far = moved(2, offs[i])
+        mail.await_recv(role2(i, 2), blk(far, 0), a_minus)
+        mail.await_recv(role2(i, 3), blk(far, 1), a_plus)
+        to_partner(3, i)
+
+    own = moved(0, 0)
+    mail.send(base + 0, blk(own), blk(own), b_plus)
+    mail.send(base + 1, blk(own), blk(own), b_minus)
+    line_out(0)
+    to_partner(0, 0)
+    low, high = moved(0, -1), moved(0, 1)
+    mail.await_recv(base + 0, blk(low), b_minus)
+    mail.send(base + 2, blk(low, 0), blk(low, 0), b_plus)
+    line_out(1)
+    to_partner(0, 1)
+    mail.await_recv(base + 1, blk(high), b_plus)
+    mail.send(base + 3, blk(high, 1), blk(high, 1), b_minus)
+    line_out(2)
+    to_partner(0, 2)
+    line_relay(0)
+    far = moved(0, 2)
+    mail.await_recv(base + 2, blk(far, 0), b_minus)
+    mail.await_recv(base + 3, blk(far, 1), b_plus)
+    line_out(3)
+    to_partner(0, 3)
+    line_relay(1)
+    line_relay(2)
+    line_far(0)
+    line_relay(3)
+    line_far(1)
+    line_far(2)
+    line_far(3)
+
+    def from_partner(ia, ib):
+        owner = moved(offs[ib], offs[ia], 1)
+        mail.await_recv(base + 20 + ia * 4 + ib, blk(owner), partner)
+
+    for ia in range(4):
+        for ib in range(4):
+            from_partner(ia, ib)
+
+
+SCATTER_ROLES = 17
+
+
+def reduce_rows(mail, base, product, width, xs, xr, sums, acc, near, mid, last, swap_out, swap_in):
+    x, z, c = place()
+    a = (1 - c) * z + c * x
+    b = (1 - c) * x + c * z
+    partner = moved(0, 0, 1)
+    a_plus, a_minus = moved(1, 0), moved(-1, 0)
+    b_plus, b_minus = moved(0, 1), moved(0, -1)
+    steps = (2, 1, 3, 0)
+
+    def set_chips(k, cc):
+        return [(1 - cc) * (j * 4 + k) + cc * (k * 4 + j) for j in range(4)]
+
+    def partner_part(idx):
+        k = (b + steps[idx]) % 4
+        product(set_chips(k, 1 - c), 1 - c, xs.at[idx], None)
+        mail.send(base + idx, xs.at[idx], xr.at[idx], partner)
+
+    def own_part(idx, out):
+        k = (a + steps[idx]) % 4
+        mail.await_recv(base + idx, xr.at[idx], partner)
+        product(set_chips(k, c), c, out, xr.at[idx])
+
+    lo, hi = pl.ds(0, 128), pl.ds(128, 128)
+    partner_part(0)
+    partner_part(1)
+    own_part(0, sums.at[0])
+    mail.send(base + 4, sums.at[0, lo], near.at[0, lo], a_plus)
+    mail.send(base + 5, sums.at[0, hi], near.at[1, hi], a_minus)
+    partner_part(2)
+    own_part(1, sums.at[1])
+    mail.send(base + 6, sums.at[1, hi], mid.at[0, hi], a_plus)
+    partner_part(3)
+    own_part(2, sums.at[2])
+    mail.send(base + 7, sums.at[2, lo], mid.at[1, lo], a_minus)
+    mail.await_recv(base + 4, near.at[0, lo], a_minus)
+    sums[1, lo] = (sums[1, lo].astype(jnp.float32) + near[0, lo].astype(jnp.float32)).astype(jnp.bfloat16)
+    mail.send(base + 8, sums.at[1, lo], mid.at[0, lo], a_plus)
+    mail.await_recv(base + 5, near.at[1, hi], a_plus)
+    sums[2, hi] = (sums[2, hi].astype(jnp.float32) + near[1, hi].astype(jnp.float32)).astype(jnp.bfloat16)
+    mail.send(base + 9, sums.at[2, hi], mid.at[1, hi], a_minus)
+    own_part(3, acc)
+    mail.await_recv(base + 6, mid.at[0, hi], a_minus)
+    mail.await_recv(base + 7, mid.at[1, lo], a_plus)
+    mail.await_recv(base + 8, mid.at[0, lo], a_minus)
+    mail.await_recv(base + 9, mid.at[1, hi], a_plus)
+
+    def chunk(j, low, size):
+        return pl.ds(pl.multiple_of(j * 64 + low, 32), size)
+
+    def chunk_sum(j, low, size):
+        at = chunk(j, low, size)
+        return acc[at] + mid[0, at].astype(jnp.float32) + mid[1, at].astype(jnp.float32)
+
+    far, up, down, own = (b + 2) % 4, (b + 1) % 4, (b + 3) % 4, b
+    q = sums.at[3]
+    q[chunk(far, 0, 64)] = chunk_sum(far, 0, 64).astype(jnp.bfloat16)
+    mail.send(base + 10, q.at[chunk(far, 0, 32)], last.at[0], b_plus)
+    mail.send(base + 11, q.at[chunk(far, 32, 32)], last.at[1], b_minus)
+    q[chunk(up, 32, 32)] = chunk_sum(up, 32, 32).astype(jnp.bfloat16)
+    mail.send(base + 12, q.at[chunk(up, 32, 32)], last.at[2], b_plus)
+    q[chunk(down, 0, 32)] = chunk_sum(down, 0, 32).astype(jnp.bfloat16)
+    mail.send(base + 13, q.at[chunk(down, 0, 32)], last.at[3], b_minus)
+    mail.await_recv(base + 10, last.at[0], b_minus)
+    q[chunk(up, 0, 32)] = (chunk_sum(up, 0, 32) + last[0].astype(jnp.float32)).astype(jnp.bfloat16)
+    mail.send(base + 14, q.at[chunk(up, 0, 32)], last.at[4], b_plus)
+    mail.await_recv(base + 11, last.at[1], b_plus)
+    q[chunk(down, 32, 32)] = (chunk_sum(down, 32, 32) + last[1].astype(jnp.float32)).astype(jnp.bfloat16)
+    mail.send(base + 15, q.at[chunk(down, 32, 32)], last.at[5], b_minus)
+    top, bottom = chunk_sum(own, 0, 32), chunk_sum(own, 32, 32)
+    mail.await_recv(base + 12, last.at[2], b_minus)
+    mail.await_recv(base + 13, last.at[3], b_plus)
+    mail.await_recv(base + 14, last.at[4], b_minus)
+    mail.await_recv(base + 15, last.at[5], b_plus)
+    top = top + last[3].astype(jnp.float32) + last[4].astype(jnp.float32)
+    bottom = bottom + last[2].astype(jnp.float32) + last[5].astype(jnp.float32)
+    is_first = c == 0
+    swap_out[...] = jnp.where(is_first, bottom, top)
+    mail.send(base + 16, swap_out, swap_in, partner)
+    mine = jnp.where(is_first, top, bottom)
+    mail.await_recv(base + 16, swap_in, partner)
+    return mine
+
+
+TAIL_ROLES = SCATTER_ROLES * 2 + GATHER_ROLES
+
+
+def tail_kernel(
+    heads_ref, w_out_hbm, gain_ref, w_gu_hbm, w_down_hbm, attn_ref, block_ref,
+    w_out, w_gu, w_down, load_sems, send_sems, recv_sems,
+    xs, xr, sums, acc, near, mid, last, swap_out, swap_in,
+    xs2, xr2, sums2, near2, mid2, last2, swap_out2, swap_in2,
+    ff_buf, hidden,
+):
+    x, z, c = place()
+    loads = [
+        pltpu.make_async_copy(w_out_hbm, w_out, load_sems.at[0]),
+        pltpu.make_async_copy(w_gu_hbm, w_gu, load_sems.at[1]),
+        pltpu.make_async_copy(w_down_hbm, w_down, load_sems.at[2]),
+    ]
+    for load in loads:
+        load.start()
+    greet([
+        {"hid": moved(1, 0)}, {"hid": moved(-1, 0)}, {"hid": moved(0, 1)},
+        {"hid": moved(0, -1)}, {"hid": moved(0, 0, 1)},
+    ])
+    mail = Mail(send_sems, recv_sems)
+    width = w_out.shape[1] // 2
+    step = width // 2
+
+    def product_of(lhs, weight):
+        def product(chips, half, out, other):
+            rows = jnp.concatenate(
+                [lhs[pl.ds(pl.multiple_of(chip * 64, 64), 64), :] for chip in chips], axis=0
+            )
+            for n in range(2):
+                at = pl.ds(n * step, step)
+                cols = pl.ds(pl.multiple_of(half * width + n * step, 128), step)
+                value = jnp.dot(rows, weight[:, cols], preferred_element_type=jnp.float32)
+                if other is not None:
+                    value = value + other[:, at].astype(jnp.float32)
+                out[:, at] = value.astype(out.dtype)
+        return product
+
+    mine_at = pl.ds(pl.multiple_of(c * width, 128), width)
+    other_at = pl.ds(pl.multiple_of((1 - c) * width, 128), width)
+
+    loads[0].wait()
+    mine = reduce_rows(
+        mail, 0, product_of(heads_ref, w_out), width,
+        xs, xr, sums, acc, near, mid, last, swap_out, swap_in,
+    )
+    other = swap_in[...]
+    attn_ref[:, mine_at] = mine.astype(jnp.bfloat16)
+    attn_ref[:, other_at] = other.astype(jnp.bfloat16)
+    total = jnp.sum(mine * mine, axis=1, keepdims=True) + jnp.sum(other * other, axis=1, keepdims=True)
+    scale = lax.rsqrt(total / (2 * width) + EPS)
+    own_rows = pl.ds(pl.multiple_of(moved(0, 0) * 32, 32), 32)
+    ff_buf[own_rows, mine_at] = (mine * scale * gain_ref[:, mine_at]).astype(jnp.bfloat16)
+    ff_buf[own_rows, other_at] = (other * scale * gain_ref[:, other_at]).astype(jnp.bfloat16)
+
+    gather_rows(mail, SCATTER_ROLES, ff_buf, 32)
+
+    units = w_down.shape[0]
+    loads[1].wait()
+
+    @pl.loop(0, 4)
+    def _(i):
+        at = pl.ds(pl.multiple_of(i * 256, 256), 256)
+        rows = ff_buf[at, :]
+        contract = (((1,), (1,)), ((), ()))
+        gate = lax.dot_general(rows, w_gu[pl.ds(0, units), :], contract, preferred_element_type=jnp.float32)
+        up = lax.dot_general(rows, w_gu[pl.ds(units, units), :], contract, preferred_element_type=jnp.float32)
+        hidden[at, :] = (jax.nn.silu(gate) * up).astype(jnp.bfloat16)
+
+    loads[2].wait()
+    mine = reduce_rows(
+        mail, SCATTER_ROLES + GATHER_ROLES, product_of(hidden, w_down), width,
+        xs2, xr2, sums2, acc, near2, mid2, last2, swap_out2, swap_in2,
+    )
+    block_ref[:, mine_at] = mine.astype(jnp.bfloat16)
+    block_ref[:, other_at] = swap_in2[...].astype(jnp.bfloat16)
+    mail.drain()
+
+
+def tail(heads_out, w_out, gain_ff, w_gu, w_down):
+    tok_grp = heads_out.shape[0]
+    width = w_out.shape[1]
+    half = width // 2
+    units = w_down.shape[0]
+    bf16, f32 = jnp.bfloat16, jnp.float32
+    vmem = pl.BlockSpec(memory_space=pltpu.VMEM)
+    anywhere = pl.BlockSpec(memory_space=pl.ANY)
+
+    def travel():
+        return [
+            pltpu.VMEM((4, 256, half), bf16), pltpu.VMEM((4, 256, half), bf16),
+            pltpu.VMEM((4, 256, half), bf16),
+        ]
+
+    def landing():
+        return [
+            pltpu.VMEM((2, 256, half), bf16), pltpu.VMEM((2, 256, half), bf16),
+            pltpu.VMEM((6, 32, half), bf16), pltpu.VMEM((32, half), f32), pltpu.VMEM((32, half), f32),
+        ]
+
+    return pl.pallas_call(
+        tail_kernel,
+        out_shape=(jax.ShapeDtypeStruct((32, width), bf16), jax.ShapeDtypeStruct((32, width), bf16)),
+        in_specs=[vmem, anywhere, vmem, anywhere, anywhere],
+        out_specs=(vmem, vmem),
+        scratch_shapes=[
+            pltpu.VMEM(w_out.shape, bf16), pltpu.VMEM(w_gu.shape, bf16), pltpu.VMEM(w_down.shape, bf16),
+            pltpu.SemaphoreType.DMA((3,)), pltpu.SemaphoreType.DMA((TAIL_ROLES,)),
+            pltpu.SemaphoreType.DMA((TAIL_ROLES,)),
+            *travel(), pltpu.VMEM((256, half), f32), *landing(),
+            *travel(), *landing(),
+            pltpu.VMEM((tok_grp, width), bf16), pltpu.VMEM((tok_grp, units), bf16),
+        ],
+        compiler_params=pltpu.CompilerParams(
+            collective_id=0, has_side_effects=True, vmem_limit_bytes=66000000
+        ),
+        name="tail",
+    )(heads_out, w_out, gain_ff.reshape(1, width), w_gu, w_down)
 
 
 def per_device(
@@ -113,27 +453,9 @@
         partial_value,
     )
     heads_out = (partial_value[2] / partial_value[1][..., None]).astype(jnp.bfloat16)
-    out_weight = w_out.reshape(head_count, HD, model_width)
-    projected_out = jnp.einsum(
-        "htd,hdm->tm", heads_out, out_weight, preferred_element_type=jnp.float32
-    )
-    summed = lax.psum(projected_out.astype(jnp.bfloat16), "hid").astype(jnp.float32)
-    hid_index = lax.axis_index("hid")
-    attn_out = lax.dynamic_slice_in_dim(summed, hid_index * tok_dev, tok_dev, 0).astype(
-        jnp.bfloat16
-    )
-    ff_in = rms_scale(summed, gain_ff).astype(jnp.bfloat16)
     unit_count = w_gate_up.shape[2]
-    gate_up = jnp.dot(
-        ff_in, w_gate_up.reshape(model_width, 2 * unit_count), preferred_element_type=jnp.float32
-    )
-    hidden = (jax.nn.silu(gate_up[:, :unit_count]) * gate_up[:, unit_count:]).astype(jnp.bfloat16)
-    block_out = lax.psum_scatter(
-        jnp.dot(hidden, w_down, preferred_element_type=jnp.float32).astype(jnp.bfloat16),
-        "hid",
-        scatter_dimension=0,
-        tiled=True,
-    )
+    w_gu = jnp.transpose(w_gate_up, (1, 2, 0)).reshape(2 * unit_count, model_width)
+    attn_out, block_out = tail(heads_out.reshape(tok_grp, head_cols), w_out, gain_ff, w_gu, w_down)
     return (attn_out, block_out)
 
 

time: 457 us -> 320 us (0.70)
  waiting for transfers between devices: 261 us -> 58 us
  Pallas kernels: 0 us -> 101 us
  matrix products: 52.9 us -> 28.5 us
    psum x1 -> x0, waiting for transfers between devices: 119 us -> none  [per_device(): lax.psum(projected_out.astype(jnp.bfloat16), 'hid').astype(jnp.float32)]
    pallas_call x0 -> x1, Pallas kernels: none -> 101 us  [tail(): pl.pallas_call(tail_kernel, out_shape=(jax.ShapeDtypeStruct((32, width),...]
    reduce_scatter x1 -> x0, waiting for transfers between devices: 85 us -> none  [per_device(): lax.psum_scatter(jnp.dot(hidden, w_down, preferred_element_type=jnp.float...]
    dot_general x3 -> x0, matrix products: 22.2 us -> none  [the longest x1 9.09 us: per_device(): jnp.dot(ff_in, w_gate_up.reshape(model_width, 2 * unit_count), preferred_...]
    reduce_sum x2 -> x1, other arithmetic: 6.09 us -> 1.34 us  [rms_scale(): jnp.mean(matrix * matrix, axis=-1, keepdims=True) + EPS]
    unnamed x20 -> x18, local copies, waits for them, and re-layouts: 35.3 us -> 34 us
  transfers between devices with their start and end apart: 4 -> 2, of which waited for: 3 -> 1; matrix products, arithmetic and copies ran while one was open for 15% -> 19% of each run, Pallas kernels for 0% -> 0%
where the time goes in v1:
time: 320 us; the launch traced here: 319 us
  Pallas kernels  101 us (32%)
  waiting for transfers between devices  58 us (18%)
  local copies, waits for them, and re-layouts  57.1 us (18%)
  blocking collectives  49.2 us (15%)
  matrix products  28.5 us (9%)
  between operations  17.4 us (5%)
  other arithmetic  6.74 us (2%)
    pallas_call x1, Pallas kernels, tail(): pl.pallas_call(tail_kernel, out_shape=(jax.ShapeDtypeStruct((32, width),...  101 us
    all_gather x1, waiting for transfers between devices, per_device(): shard_rows = lax.all_gather(heads_cache, 'req', axis=0, tiled=True)  58 us
    all_to_all x1, blocking collectives, per_device(): lax.all_to_all(prefix_cache[0], 'hid', split_axis=2, concat_axis=0, tiled...  49.2 us
    unnamed x18, local copies, waits for them, and re-layouts  34 us
    dot_general x1, matrix products, per_device(): jnp.dot(shard_rows[:, :width_in], joint_weight, preferred_element_type=jn...  15.6 us
    another operation x1, local copies, waits for them, and re-layouts  11 us
    all_to_all x1, local copies, waits for them, and re-layouts, per_device(): lax.all_to_all(prefix_cache[0], 'hid', split_axis=2, concat_axis=0, tiled...  8.17 us
  transfers between devices with their start and end apart: 2, of which 1 were waited for; matrix products, arithmetic and copies ran while one was open for 19% of the time, Pallas kernels for 0%

profile of v1, /device:TPU:1, one launch (start us, length us, event | category | flops | bytes accessed | tf_op | source)
XLA Modules:
  0.0 319.0 jit_solution(8943481630801770805)
XLA Ops:
  7.2 0.0 copy-start
  7.2 0.0 copy-start.2
  7.2 0.0 all-gather.3.cloned.1.call-start
  7.2 1.3 fusion.33
  8.6 1.2 fusion.35
  9.8 1.9 convolution_convert_fusion
  11.7 0.9 pad_maximum_fusion
  12.6 0.0 all-gather.3.cloned.1.call-update
  12.6 0.0 all-gather.5.cloned.1.call-start
  12.6 0.0 copy-done.2
  12.6 6.7 %copy.35 = bf16[1,64,2,7168]{1,2,3,0:T(2,128)(2,1)} copy(bf16[1,64,2,7168]{3,2,1,0:T(2,128)(2,1)S(1)} %copy-done.2) | data formatting | bytes 3670016 | tf_op args[9]
  19.4 7.1 %bitcast_bitcast_fusion = bf16[7168,2,64]{2,1,0:T(2,128)(2,1)} fusion(bf16[1,64,2,7168]{1,2,3,0:T(2,128)(2,1)} %copy.35), kind=kLoop, calls=%fused_computation.52 | loop fusion | bytes 3670016
  26.5 8.2 %reshape.139 = bf16[32,2,14336]{2,1,0:T(2,128)(2,1)S(1)} reshape(bf16[7168,2,64]{2,1,0:T(2,128)(2,1)} %bitcast_bitcast_fusion) | data formatting | bytes 3670016
  34.6 49.2 %all_to_all.18 = bf16[32,2,14336]{2,1,0:T(2,128)(2,1)} all-to-all(bf16[32,2,14336]{2,1,0:T(2,128)(2,1)S(1)} %reshape.139), channel_id=1, replica_groups=mesh['req'=4,'hid'=32] {'hid'}, dimensions={0} | all-to-all | bytes 3670016 | tf_op jit(solution)/shard_map/all_to_all | solution.py:441
  83.8 8.8 %reshape.140 = bf16[7168,2,64]{2,1,0:T(2,128)(2,1)} reshape(bf16[32,2,14336]{2,1,0:T(2,128)(2,1)} %all_to_all.18) | data formatting | bytes 3670016
  92.6 0.0 copy-start.4
  92.6 0.0 copy-start.5
  92.6 0.0 copy-start.6
  92.6 0.0 copy-start.3
  92.6 8.2 %copy.36 = bf16[64,2,32,224]{3,0,2,1:T(8,128)(2,1)} copy(bf16[64,2,32,224]{0,1,3,2:T(2,128)(2,1)} %bitcast.43) | data formatting | bytes 3670016 | tf_op jit(solution)/shard_map/all_to_all | solution.py:441
  100.8 0.0 all-gather.5.cloned.1.call-update
  100.8 0.0 copy-done.4
  100.8 0.6 dynamic_slice.14
  103.3 0.0 copy-done.5
  103.3 0.6 dynamic_slice.15
  105.2 0.0 copy-done.6
  105.2 0.2 reduce-window.8
  105.4 0.0 copy-done.3
  105.4 0.6 reshape.137.gain_ref
  106.0 0.1 convert_reduce_fusion
  106.1 0.0 all-gather.3.cloned.1.call-done
  106.1 15.6 %fusion.42 = (bf16[1024,672]{0,1:T(8,128)(2,1)S(1)}, f32[1024,672]{0,1:T(8,128)S(1)}) fusion(bf16[7168,672]{0,1:T(8,128)(2,1)} %bitcast.52, bf16[1024,7296]{1,0:T(8,128)(2,1)} %all-gather.3.cloned.1.call-done), kind=kOutput, calls=%fused_computation.50 | convolution fusion | flops 9865691136 | bytes 28442624 | tf_op jit(solution)/shard_map/dot_general | solution.py:423
  121.7 0.0 copy-done
  121.7 1.2 fusion.32
  123.0 1.1 fusion.43
  124.1 0.6 fusion.25
  124.7 0.8 fusion.29
  125.5 58.0 %all-gather.5.cloned.1.call-done = bf16[8192,2,224]{2,0,1:T(8,128)(2,1)} async-done(((bf16[2048,2,224]{2,0,1:T(8,128)(2,1)}), bf16[8192,2,224]{2,0,1:T(8,128)(2,1)}) %all-gather.5.cloned.1.call-update) | async-done | bytes 7340048 | tf_op jit(solution)/shard_map/all_gather | solution.py:443
  183.5 23.1 %conditional.1 = (f32[1,1024]{1,0:T(1,128)S(1)}, f32[1,1024,224]{2,1,0:T(8,128)S(1)}) conditional(s32[]{:T(128)} %convert_element_type.30, (f32[1,1024]{1,0:T(1,128)S(1)}, f32[1,1024,224]{1,2,0:T(8,128)S(1)}) %tuple.45, (s32[]{:T(128)}, bf16[8192,2,224]{2,0,1:T(8,128)(2,1)}, bf16[1024,224]{0,1:T(8,128)(2,1)S(1)}, f32[1024]{0:T(1024)S(1)}, ...), branch_computations={%region_5.6_spmd, %region_6.9_spmd} | conditional | flops 1896517632 | bytes 79429776 | solution.py:449
  183.5 11.0 %copy.37 = bf16[8192,2,224]{0,2,1:T(8,128)(2,1)} copy(bf16[8192,2,224]{2,0,1:T(8,128)(2,1)} %get-tuple-element.113) | data formatting | bytes 14680064 | tf_op jit(solution)/shard_map
  195.1 2.5 multiply_reduce_fusion
  197.6 0.0 copy-start.1
  197.6 1.4 fusion.1
  199.0 1.8 copy-done.1
  200.9 5.4 %fusion.12 = f32[1,1024,224]{1,2,0:T(8,128)S(1)} fusion(f32[2048,1024]{1,0:T(8,128)} %copy-done.1, f32[1024]{0:T(1024)S(1)} %get-tuple-element.124, bf16[8192,2,224]{0,2,1:T(8,128)(2,1)} %copy.37, s32[]{:T(128)S(6)} %select_n.13, s32[]{:T(128)S(6)} %add.41, f32[1,1024,224]{1,2,0:T(8,128)S(1)} %get-tuple-element.75, f32[1024]{0:T(1024)S(1)} %get-tuple-element.122, ...), kind=kOutput, calls=%fused_computation.9 | convolution fusion | flops 946503680 | bytes 11153416 | tf_op jit(solution)/shard_map/cond/branch_1_fun/htp,phd->htd/dot_general | solution.py:30
  206.3 0.3 copy.42
  206.6 1.0 fusion.36.heads_ref
  207.6 101.2 %tail.1 = (bf16[32,3584]{1,0:T(8,128)(2,1)}, bf16[32,3584]{1,0:T(8,128)(2,1)}) custom-call(bf16[1024,224]{1,0:T(8,128)(2,1)} %fusion.36.heads_ref, bf16[224,3584]{1,0:T(8,128)(2,1)} %w_out_hbm.1, f32[1,3584]{1,0:T(1,128)} %reshape.137.gain_ref, bf16[896,3584]{1,0:T(8,128)(2,1)} %bitcast.45, bf16[448,3584]{1,0:T(8,128)(2,1)} %w_down_hbm.1), custom_call_target="tpu_custom_call" | custom-call | tf_op jit(solution)/shard_map/tail/pallas_call | solution.py:378
  308.9 1.6 copy.49
  310.5 1.6 copy.50
  (3 shorter events, 0.0 us)
Async XLA Ops:
  7.2 114.6 %copy-start = (bf16[128,224]{0,1:T(8,128)(2,1)S(1)}, bf16[128,224]{0,1:T(8,128)(2,1)}, u32[]{:S(2)}) copy-start(bf16[128,224]{0,1:T(8,128)(2,1)} %param.19) | copy-start | bytes 172036
  7.2 5.5 %copy-start.2 = (bf16[1,64,2,7168]{3,2,1,0:T(2,128)(2,1)S(1)}, bf16[1,64,2,7168]{3,2,1,0:T(2,128)(2,1)}, u32[]{:S(2)}) copy-start(bf16[1,64,2,7168]{3,2,1,0:T(2,128)(2,1)} %param.24) | copy-start | bytes 5505028
  7.2 98.9 %all-gather.3.cloned.1.call-start = ((), (), s32[]{:S(2)}) async-start(), calls=%async_computation.1 | async-start | bytes 15409152 | tf_op jit(solution)/shard_map/all_gather | solution.py:422
  12.6 170.9 %all-gather.5.cloned.1.call-start = ((), (), s32[]{:S(2)}) async-start(), calls=%async_computation.2 | async-start | bytes 10485760 | tf_op jit(solution)/shard_map/all_gather | solution.py:443
  92.6 8.2 %copy-start.4 = (s32[4]{0:T(128)S(1)}, s32[4]{0:T(128)}, u32[]{:S(2)}) copy-start(s32[4]{0:T(128)} %param.26) | copy-start | bytes 52
  92.6 10.8 %copy-start.5 = (s32[3]{0:T(128)S(1)}, s32[3]{0:T(128)}, u32[]{:S(2)}) copy-start(s32[3]{0:T(128)} %param.25) | copy-start | bytes 40
  92.6 12.6 %copy-start.6 = (s32[1,6]{1,0:T(1,128)S(1)}, s32[1,6]{1,0:T(1,128)}, u32[]{:S(2)}) copy-start(s32[1,6]{1,0:T(1,128)} %param.27) | copy-start | bytes 76
  92.6 12.8 %copy-start.3 = (f32[3584]{0:T(1024)S(1)}, f32[3584]{0:T(1024)}, u32[]{:S(2)}) copy-start(f32[3584]{0:T(1024)} %param.21) | copy-start | bytes 43012
  197.6 3.2 %copy-start.1 = (f32[2048,1024]{1,0:T(8,128)}, f32[2048,1024]{1,0:T(8,128)S(1)}, u32[]{:S(2)}) copy-start(f32[2048,1024]{1,0:T(8,128)S(1)} %get-tuple-element.125) | copy-start | bytes 25165828 | tf_op jit(solution)/shard_map/cond
Sparse Core Ops, SparseCore 0:
  12.7 86.9 all-gather.2
  101.4 82.0 all-gather.4

commit v2 on v1

--- a/solution.py
+++ b/solution.py
@@ -15,48 +15,6 @@
     return matrix * lax.rsqrt(jnp.mean(matrix * matrix, axis=-1, keepdims=True) + EPS) * gain_vec
 
 
-def prefix_part(queries, kv_block):
-    span_len = kv_block.shape[0]
-    head_count = queries.shape[1]
-    head_size = queries.shape[2]
-    cached_k = kv_block[:, 0].reshape(span_len, head_count, head_size)
-    cached_v = kv_block[:, 1].reshape(span_len, head_count, head_size)
-    scores = jnp.einsum(
-        "thd,phd->htp", queries, cached_k, preferred_element_type=jnp.float32
-    ) * head_size ** (-0.5)
-    row_max = jnp.max(scores, axis=-1)
-    expos = jnp.exp(scores - row_max[..., None])
-    row_sum = jnp.sum(expos, axis=-1)
-    weighted = jnp.einsum(
-        "htp,phd->htd", expos.astype(jnp.bfloat16), cached_v, preferred_element_type=jnp.float32
-    )
-    return (row_max, row_sum, weighted)
-
-
-def suffix_part(queries, suffix_keys, suffix_vals, allowed):
-    head_size = queries.shape[2]
-    scores = jnp.einsum(
-        "thd,shd->hts", queries, suffix_keys, preferred_element_type=jnp.float32
-    ) * head_size ** (-0.5)
-    scores = jnp.where(allowed[None], scores, -jnp.inf)
-    row_max = jnp.max(scores, axis=-1)
-    expos = jnp.exp(scores - row_max[..., None])
-    row_sum = jnp.sum(expos, axis=-1)
-    weighted = jnp.einsum(
-        "hts,shd->htd", expos.astype(jnp.bfloat16), suffix_vals, preferred_element_type=jnp.float32
-    )
-    return (row_max, row_sum, weighted)
-
-
-def combine(first_part, second_part):
-    joint_max = jnp.maximum(first_part[0], second_part[0])
-    first_factor = jnp.exp(first_part[0] - joint_max)
-    second_factor = jnp.exp(second_part[0] - joint_max)
-    joint_sum = first_part[1] * first_factor + second_part[1] * second_factor
-    joint_acc = first_part[2] * first_factor[..., None] + second_part[2] * second_factor[..., None]
-    return (joint_max, joint_sum, joint_acc)
-
-
 MESH = pl.DeviceIdType.MESH
 NX, NZ = 4, 4
 
@@ -108,7 +66,7 @@
 GATHER_ROLES = 36
 
 
-def gather_rows(mail, base, buf, rows, on_pair=None):
+def gather_rows(mail, base, buf, rows):
     half = rows // 2
     x, z, c = place()
 
@@ -165,18 +123,26 @@
     line_out(2)
     to_partner(0, 2)
     line_relay(0)
+    yield "relay0"
     far = moved(0, 2)
     mail.await_recv(base + 2, blk(far, 0), b_minus)
     mail.await_recv(base + 3, blk(far, 1), b_plus)
     line_out(3)
     to_partner(0, 3)
     line_relay(1)
+    yield "relay1"
     line_relay(2)
+    yield "relay2"
     line_far(0)
+    yield "far0"
     line_relay(3)
+    yield "relay3"
     line_far(1)
+    yield "far1"
     line_far(2)
+    yield "far2"
     line_far(3)
+    yield "far3"
 
     def from_partner(ia, ib):
         owner = moved(offs[ib], offs[ia], 1)
@@ -330,7 +296,8 @@
     ff_buf[own_rows, mine_at] = (mine * scale * gain_ref[:, mine_at]).astype(jnp.bfloat16)
     ff_buf[own_rows, other_at] = (other * scale * gain_ref[:, other_at]).astype(jnp.bfloat16)
 
-    gather_rows(mail, SCATTER_ROLES, ff_buf, 32)
+    for _ in gather_rows(mail, SCATTER_ROLES, ff_buf, 32):
+        pass
 
     units = w_down.shape[0]
     loads[1].wait()
@@ -395,6 +362,205 @@
     )(heads_out, w_out, gain_ff.reshape(1, width), w_gu, w_down)
 
 
+FRONT_BLOCKS = 36
+WINDOW = 768
+
+
+def front_kernel(
+    owner_ref, lengths_ref, tokens_ref, gain_ref, down_ref, up_ref, w_hbm, cache_hbm, heads_ref,
+    w_qkv, rows_buf, load_sems, send_sems, recv_sems,
+    first_0, first_1, second_0, second_1, pass_0, pass_1, split_0, split_1,
+    prefix, qkv,
+):
+    x, z, c = place()
+    hid = lax.axis_index("hid")
+    req = lax.axis_index("req")
+    lower, upper = (req + 3) % 4, (req + 1) % 4
+    width = tokens_ref.shape[1]
+    bf16, f32 = jnp.bfloat16, jnp.float32
+    first, second = (first_0, first_1), (second_0, second_1)
+    passed, split = (pass_0, pass_1), (split_0, split_1)
+
+    loads = []
+    for k in range(2):
+        for half in range(2):
+            copy = pltpu.make_async_copy(
+                cache_hbm.at[pl.ds(half * 32 + k * 16, 16)], first[k].at[half], load_sems.at[1 + 2 * k + half]
+            )
+            copy.start()
+            loads.append(copy)
+    w_load = pltpu.make_async_copy(w_hbm, w_qkv, load_sems.at[0])
+    w_load.start()
+
+    peers = [{"hid": (hid + d) % 32} for d in range(1, 32)] + [{"req": lower}, {"req": upper}]
+    barrier = pltpu.get_barrier_semaphore()
+    for peer in peers:
+        pl.semaphore_signal(barrier, inc=1, device_id=peer, device_id_type=MESH)
+    matrix = tokens_ref[...].astype(f32)
+    normed = rms_scale(matrix, gain_ref[...]).astype(bf16)
+    own_rows = pl.ds(pl.multiple_of(hid * 32, 32), 32)
+    rows_buf[own_rows, pl.ds(0, width)] = normed
+    latent = jnp.dot(normed, down_ref[...], preferred_element_type=f32)
+    rows_buf[own_rows, pl.ds(width, 128)] = latent.astype(bf16)
+    pl.semaphore_wait(barrier, len(peers))
+
+    mail = Mail(send_sems, recv_sems)
+    y_base = GATHER_ROLES
+    deal_base = y_base + 8
+
+    def y_copy(role, src, dst, to):
+        return pltpu.make_async_remote_copy(
+            src_ref=src, dst_ref=dst, send_sem=send_sems.at[role], recv_sem=recv_sems.at[role],
+            device_id={"req": to}, device_id_type=MESH,
+        )
+
+    def y_send(role, src, dst, to):
+        copy = y_copy(role, src, dst, to)
+        copy.start()
+        mail.sent.append(copy)
+
+    def y_start():
+        for k in range(2):
+            y_send(y_base + k, cache_hbm.at[pl.ds(k * 16, 16)], first[k].at[2], lower)
+            y_send(y_base + 2 + k, cache_hbm.at[pl.ds(32 + k * 16, 16)], first[k].at[3], upper)
+
+    def y_pass(k):
+        loads[2 * k].wait()
+        loads[2 * k + 1].wait()
+        y_copy(y_base + k, first[k].at[2], first[k].at[2], upper).wait_recv()
+        y_copy(y_base + 2 + k, first[k].at[3], first[k].at[3], lower).wait_recv()
+        passed[k][0] = first[k][jnp.where(owner_ref[lower] == req, 1, 2)]
+        y_send(y_base + 4 + k, passed[k].at[0], second[k].at[0], lower)
+        passed[k][1] = first[k][jnp.where(owner_ref[upper] == req, 0, 3)]
+        y_send(y_base + 6 + k, passed[k].at[1], second[k].at[1], upper)
+
+    def deal(k):
+        y_copy(y_base + 4 + k, second[k].at[0], second[k].at[0], upper).wait_recv()
+        y_copy(y_base + 6 + k, second[k].at[1], second[k].at[1], lower).wait_recv()
+        away = (owner_ref[req] - req + 4) % 4
+        late_a = jnp.full((1, 1, 1), (away >= 2).astype(jnp.int32)) > 0
+        late_b = jnp.full((1, 1, 1), jnp.logical_or(away == 1, away == 2).astype(jnp.int32)) > 0
+        half_a = jnp.where(late_a, second[k][jnp.where(away == 2, 0, 1)], first[k][jnp.where(away == 0, 0, 2)])
+        half_b = jnp.where(late_b, second[k][jnp.where(away == 1, 0, 1)], first[k][jnp.where(away == 0, 1, 3)])
+        r = lax.broadcasted_iota(jnp.int32, (32, 32), 0)
+        s = lax.broadcasted_iota(jnp.int32, (32, 32), 1)
+        sort = (s == jnp.where(r < 16, 2 * r, 2 * r - 31)).astype(bf16)
+        zeros = jnp.zeros((16, 256 - HD), bf16)
+        for half, value in enumerate((half_a, half_b)):
+            planes = jnp.dot(sort, value.reshape(32, width), preferred_element_type=f32).astype(bf16)
+            for kv in range(2):
+                for h in range(32):
+                    piece = planes[kv * 16:(kv + 1) * 16, h * HD:(h + 1) * HD]
+                    split[k][h, kv, pl.ds(half * 16, 16), :] = jnp.concatenate([piece, zeros], axis=1)
+
+        landing = prefix.at[:, pl.ds(pl.multiple_of(hid * 64 + k * 32, 32), 32)]
+        for d in range(1, 32):
+            to = (hid + d) % 32
+            mail.send(deal_base + k * 31 + d - 1, split[k].at[to], landing, to)
+        prefix[:, pl.ds(pl.multiple_of(hid * 64 + k * 32, 32), 32)] = split[k][hid]
+
+    def deal_done():
+        for k in range(2):
+            for d in range(1, 32):
+                source = (hid + 32 - d) % 32
+                landing = prefix.at[:, pl.ds(pl.multiple_of(source * 64 + k * 32, 32), 32)]
+                mail.await_recv(deal_base + k * 31 + d - 1, landing, source)
+
+    y_start()
+    for stage in gather_rows(mail, 0, rows_buf, 32):
+        if stage == "relay0":
+            y_pass(0)
+        if stage == "relay2":
+            y_pass(1)
+        if stage == "far1":
+            deal(0)
+    deal(1)
+
+    w_load.wait()
+    contract = (((1,), (1,)), ((), ()))
+    pad = jnp.zeros((256, 256 - HD), bf16)
+
+    @pl.loop(0, 4)
+    def _(i):
+        at = pl.ds(pl.multiple_of(i * 256, 256), 256)
+        rows = rows_buf[at, pl.ds(0, width)]
+        for part in range(3):
+            value = lax.dot_general(
+                rows, w_qkv[pl.ds(part * HD, HD), :], contract, preferred_element_type=f32
+            )
+            if part == 0:
+                value = value + lax.dot_general(
+                    rows_buf[at, pl.ds(width, 128)], up_ref[...], contract, preferred_element_type=f32
+                )
+            qkv[part, at, :] = jnp.concatenate([value.astype(bf16), pad], axis=1)
+
+    deal_done()
+
+    ends = [lengths_ref[0, 0]]
+    for n in range(1, lengths_ref.shape[1]):
+        ends.append(ends[-1] + lengths_ref[0, n])
+    factor = HD ** (-0.5)
+
+    @pl.loop(0, 8)
+    def _(i):
+        at = pl.ds(pl.multiple_of(i * 128, 128), 128)
+        begin = jnp.maximum(i * 128 - 512, 0) // 128 * 128
+        begin = jnp.minimum(begin, 1024 - WINDOW)
+        near = pl.ds(pl.multiple_of(begin, 128), WINDOW)
+        q = qkv[0, at, :]
+        s_far = lax.dot_general(q, prefix[0], contract, preferred_element_type=f32) * factor
+        s_near = lax.dot_general(q, qkv[1, near, :], contract, preferred_element_type=f32) * factor
+        row = lax.broadcasted_iota(jnp.int32, (128, 1), 0) + i * 128
+        since = jnp.zeros((128, 1), jnp.int32)
+        for end in ends:
+            since = jnp.where(row >= end, jnp.maximum(since, end), since)
+        col = lax.broadcasted_iota(jnp.int32, (128, WINDOW), 1) + begin
+        s_near = jnp.where(jnp.logical_and(col >= since, col <= row), s_near, -jnp.inf)
+        row_max = jnp.maximum(
+            jnp.max(s_far, axis=1, keepdims=True), jnp.max(s_near, axis=1, keepdims=True)
+        )
+        e_far = jnp.exp(s_far - row_max)
+        e_near = jnp.exp(s_near - row_max)
+        row_sum = jnp.sum(e_far, axis=1, keepdims=True) + jnp.sum(e_near, axis=1, keepdims=True)
+        out = jnp.dot(e_far.astype(bf16), prefix[1], preferred_element_type=f32)
+        out = out + jnp.dot(e_near.astype(bf16), qkv[2, near, :], preferred_element_type=f32)
+        heads_ref[at, :] = (out / row_sum)[:, :HD].astype(bf16)
+
+    mail.drain()
+
+
+def front(owners, lengths, tokens, gain_in, adapt_down, up_t, w_t, cache):
+    rows, width = tokens.shape
+    tok_grp = rows * 32
+    bf16 = jnp.bfloat16
+    smem = pl.BlockSpec(memory_space=pltpu.SMEM)
+    vmem = pl.BlockSpec(memory_space=pltpu.VMEM)
+    anywhere = pl.BlockSpec(memory_space=pl.ANY)
+    roles = GATHER_ROLES + 8 + 62
+
+    def halves(count):
+        return pltpu.VMEM((count, 16, 2, width), bf16)
+
+    return pl.pallas_call(
+        front_kernel,
+        out_shape=jax.ShapeDtypeStruct((tok_grp, HD), bf16),
+        in_specs=[smem, smem, vmem, vmem, vmem, vmem, anywhere, anywhere],
+        out_specs=vmem,
+        scratch_shapes=[
+            pltpu.VMEM(w_t.shape, bf16), pltpu.VMEM((tok_grp, width + 128), bf16),
+            pltpu.SemaphoreType.DMA((5,)), pltpu.SemaphoreType.DMA((roles,)),
+            pltpu.SemaphoreType.DMA((roles,)),
+            halves(4), halves(4), halves(2), halves(2), halves(2), halves(2),
+            pltpu.VMEM((32, 2, 32, 256), bf16), pltpu.VMEM((32, 2, 32, 256), bf16),
+            pltpu.VMEM((2, 2048, 256), bf16), pltpu.VMEM((3, tok_grp, 256), bf16),
+        ],
+        compiler_params=pltpu.CompilerParams(
+            collective_id=1, has_side_effects=True, vmem_limit_bytes=66000000
+        ),
+        name="front",
+    )(owners, lengths, tokens, gain_in.reshape(1, width), adapt_down, up_t, w_t, cache)
+
+
 def per_device(
     tokens,
     gain_in,
@@ -410,53 +576,12 @@
     group_prefix,
     lengths,
 ):
-    tok_dev = tokens.shape[0]
-    width_in = tokens.shape[1]
-    head_cols = w_qkv.shape[2]
-    head_count = head_cols // HD
-    model_width = w_out.shape[1]
-    normed = rms_scale(tokens.astype(jnp.float32), gain_in).astype(jnp.bfloat16)
-    latent = jnp.dot(normed, adapt_down, preferred_element_type=jnp.float32).astype(jnp.bfloat16)
-    row_block = jnp.concatenate([normed, latent], axis=1)
-    joint_weight = w_qkv.reshape(width_in, 3 * head_cols)
-    shard_rows = lax.all_gather(row_block, "hid", axis=0, tiled=True)
-    joint = jnp.dot(shard_rows[:, :width_in], joint_weight, preferred_element_type=jnp.float32)
-    query_part = joint[:, :head_cols] + jnp.dot(
-        shard_rows[:, width_in:], adapt_up, preferred_element_type=jnp.float32
+    w_t = jnp.transpose(w_qkv, (1, 2, 0)).reshape(3 * w_qkv.shape[2], w_qkv.shape[0])
+    w_gu = jnp.transpose(w_gate_up, (1, 2, 0)).reshape(2 * w_gate_up.shape[2], w_gate_up.shape[0])
+    heads_out = front(
+        prefix_owner[group_prefix], lengths, tokens, gain_in, adapt_down, adapt_up.T, w_t, prefix_cache[0]
     )
-    projected = jnp.concatenate([query_part, joint[:, head_cols:]], axis=1).astype(jnp.bfloat16)
-    tok_grp = projected.shape[0]
-    queries = projected[:, :head_cols].reshape(tok_grp, head_count, HD)
-    suffix_keys = projected[:, head_cols : 2 * head_cols].reshape(tok_grp, head_count, HD)
-    suffix_vals = projected[:, 2 * head_cols :].reshape(tok_grp, head_count, HD)
-    request_ends = jnp.cumsum(lengths[0])
-    position = jnp.arange(tok_grp, dtype=jnp.int32)
-    request = jnp.sum((position[:, None] >= request_ends[None, :]).astype(jnp.int32), axis=1)
-    allowed = jnp.logical_and(
-        request[:, None] == request[None, :], position[None, :] <= position[:, None]
-    )
-    partial_value = suffix_part(queries, suffix_keys, suffix_vals, allowed)
-    group_index = lax.axis_index("req")
-    target = prefix_owner[group_prefix[group_index]]
-    heads_cache = lax.all_to_all(prefix_cache[0], "hid", split_axis=2, concat_axis=0, tiled=True)
-    span_len = heads_cache.shape[0]
-    shard_rows = lax.all_gather(heads_cache, "req", axis=0, tiled=True)
-    slot_count = shard_rows.shape[0] // span_len
-    inside = jnp.logical_and(target >= 0, target < slot_count)
-    chosen = lax.dynamic_slice_in_dim(
-        shard_rows, jnp.clip(target, 0, slot_count - 1) * span_len, span_len, 0
-    )
-    partial_value = lax.cond(
-        inside,
-        lambda kept: combine(kept, prefix_part(queries, chosen)),
-        lambda kept: kept,
-        partial_value,
-    )
-    heads_out = (partial_value[2] / partial_value[1][..., None]).astype(jnp.bfloat16)
-    unit_count = w_gate_up.shape[2]
-    w_gu = jnp.transpose(w_gate_up, (1, 2, 0)).reshape(2 * unit_count, model_width)
-    attn_out, block_out = tail(heads_out.reshape(tok_grp, head_cols), w_out, gain_ff, w_gu, w_down)
-    return (attn_out, block_out)
+    return tail(heads_out, w_out, gain_ff, w_gu, w_down)
 
 
 def solution(mesh):

time: 320 us -> 209 us (0.65)
  Pallas kernels: 101 us -> 202 us
  waiting for transfers between devices: 58 us -> 0 us
  local copies, waits for them, and re-layouts: 57.1 us -> 5.76 us
  blocking collectives: 49.2 us -> 0 us
  matrix products: 28.5 us -> 0 us
  between operations: 17.4 us -> 0.66 us
  other arithmetic: 6.74 us -> 0.67 us
    pallas_call x0 -> x1, Pallas kernels: none -> 101 us  [front(): pl.pallas_call(front_kernel, out_shape=jax.ShapeDtypeStruct((tok_grp, HD)...]
    all_gather x2 -> x0, waiting for transfers between devices: 58 us -> none  [the longest x1 58 us: per_device(): shard_rows = lax.all_gather(heads_cache, 'req', axis=0, tiled=True)]
    all_to_all x1 -> x0, blocking collectives: 49.2 us -> none  [per_device(): lax.all_to_all(prefix_cache[0], 'hid', split_axis=2, concat_axis=0, tiled...]
    unnamed x18 -> x4, local copies, waits for them, and re-layouts: 34 us -> 3.29 us
    dot_general x7 -> x0, matrix products: 28.5 us -> none  [the longest x1 15.6 us: per_device(): jnp.dot(shard_rows[:, :width_in], joint_weight, preferred_element_type=jn...]
    another operation x1 -> x0, local copies, waits for them, and re-layouts: 11 us -> none
    all_to_all x1 -> x0, local copies, waits for them, and re-layouts: 8.17 us -> none  [per_device(): lax.all_to_all(prefix_cache[0], 'hid', split_axis=2, concat_axis=0, tiled...]
    reduce_sum x4 -> x0, other arithmetic: 3.47 us -> none  [the longest x1 1.43 us: prefix_part(): row_sum = jnp.sum(expos, axis=-1)]
  transfers between devices with their start and end apart: 2 -> 0, of which waited for: 1 -> 0; matrix products, arithmetic and copies ran while one was open for 19% -> 0% of each run, Pallas kernels for 0% -> 0%
where the time goes in v2:
time: 209 us
  Pallas kernels  202 us (97%)
  local copies, waits for them, and re-layouts  5.76 us (3%)
    pallas_call x1, Pallas kernels, front(): pl.pallas_call(front_kernel, out_shape=jax.ShapeDtypeStruct((tok_grp, HD)...  101 us
    pallas_call x1, Pallas kernels, tail(): pl.pallas_call(tail_kernel, out_shape=(jax.ShapeDtypeStruct((32, width),...  101 us

profile of v2, /device:TPU:1, one launch (start us, length us, event | category | flops | bytes accessed | tf_op | source)
XLA Modules:
  0.0 209.2 jit_solution(13929981392585913963)
XLA Ops:
  0.6 0.0 copy-start
  0.6 0.7 compare_select_fusion
  1.3 0.0 copy-done
  1.3 1.1 gather_fusion
  2.5 1.3 reshape.18.gain_ref
  3.8 101.1 %front.1.heads_ref = bf16[1024,224]{1,0:T(8,128)(2,1)} custom-call(s32[4]{0:T(128)} %gather_fusion, s32[1,6]{1,0:T(1,128)} %lengths_ref.1, bf16[32,7168]{1,0:T(8,128)(2,1)} %tokens_ref.1, f32[1,7168]{1,0:T(1,128)} %bitcast.13, bf16[7168,128]{1,0:T(8,128)(2,1)} %down_ref.1, bf16[224,128]{1,0:T(8,128)(2,1)} %bitcast.12, bf16[672,7168]{1,0:T(8,128)(2,1)} %bitcast.9, ...), custom_call_target="tpu_custom_call" | custom-call | tf_op jit(solution)/shard_map/front/pallas_call | solution.py:544
  104.9 101.0 %tail.1 = (bf16[32,3584]{1,0:T(8,128)(2,1)}, bf16[32,3584]{1,0:T(8,128)(2,1)}) custom-call(bf16[1024,224]{1,0:T(8,128)(2,1)} %front.1.heads_ref, bf16[224,3584]{1,0:T(8,128)(2,1)} %w_out_hbm.1, f32[1,3584]{1,0:T(1,128)} %reshape.18.gain_ref, bf16[896,3584]{1,0:T(8,128)(2,1)} %bitcast.10, bf16[448,3584]{1,0:T(8,128)(2,1)} %w_down_hbm.1), custom_call_target="tpu_custom_call" | custom-call | tf_op jit(solution)/shard_map/tail/pallas_call | solution.py:345
  205.9 1.6 copy.17
  207.5 1.6 copy.18
  (1 shorter events, 0.0 us)
Async XLA Ops:
  0.6 0.7 copy-start

commit v3 on v2

v3 whole, which is shorter than its diff:
```python
import jax
import jax.numpy as jnp
from jax import lax
from jax.experimental import pallas as pl
from jax.experimental.pallas import tpu as pltpu
from jax.sharding import PartitionSpec as P

HD = 224


EPS = 1e-05


def rms_scale(matrix, gain_vec):
    return matrix * lax.rsqrt(jnp.mean(matrix * matrix, axis=-1, keepdims=True) + EPS) * gain_vec


MESH = pl.DeviceIdType.MESH
NX, NZ = 4, 4


def place():
    hid = lax.axis_index("hid")
    return hid // 8, (hid // 2) % 4, hid % 2


def moved(da, db, core_flip=0):
    x, z, c = place()
    xn = (x + 4 + (1 - c) * db + c * da) % 4
    zn = (z + 4 + (1 - c) * da + c * db) % 4
    cn = c + core_flip * (1 - 2 * c)
    return xn * 8 + zn * 2 + cn


def remote(src, dst, send, recv, hid):
    return pltpu.make_async_remote_copy(
        src_ref=src, dst_ref=dst, send_sem=send, recv_sem=recv,
        device_id={"hid": hid}, device_id_type=MESH,
    )


def greet(peers):
    barrier = pltpu.get_barrier_semaphore()
    for peer in peers:
        pl.semaphore_signal(barrier, inc=1, device_id=peer, device_id_type=MESH)
    pl.semaphore_wait(barrier, len(peers))


class Mail:
    def __init__(self, send_sems, recv_sems):
        self.send_sems, self.recv_sems, self.sent = send_sems, recv_sems, {}

    def send(self, role, src, dst, hid):
        copy = remote(src, dst, self.send_sems.at[role], self.recv_sems.at[role], hid)
        copy.start()
        self.sent[role] = copy

    def release(self, *roles):
        for role in roles:
            self.sent.pop(role).wait_send()

    def await_recv(self, role, dst, hid):
        remote(dst, dst, self.send_sems.at[role], self.recv_sems.at[role], hid).wait_recv()

    def drain(self):
        for copy in self.sent.values():
            copy.wait_send()


GATHER_ROLES = 36
OFFS = (0, -1, 1, 2)


class Gather:
    def __init__(self, mail, base, buf, rows):
        self.mail, self.base, self.buf, self.rows = mail, base, buf, rows
        self.a_plus, self.a_minus = moved(1, 0), moved(-1, 0)
        self.b_plus, self.b_minus = moved(0, 1), moved(0, -1)
        self.partner = moved(0, 0, 1)
        self.seen = set()

    def blk(self, hid, part=None):
        start = pl.multiple_of(hid * self.rows, self.rows)
        if part is None:
            return self.buf.at[pl.ds(start, self.rows)]
        half = self.rows // 2
        return self.buf.at[pl.ds(start + part * half, half)]

    def owner(self, ia, ib, from_partner=False):
        if from_partner:
            return moved(OFFS[ib], OFFS[ia], 1)
        return moved(OFFS[ia], OFFS[ib])

    def forward(self, role, block, to):
        self.mail.send(self.base + role, block, block, to)

    def to_partner(self, ia, ib):
        self.forward(20 + ia * 4 + ib, self.blk(self.owner(ia, ib)), self.partner)

    def from_partner(self, *places):
        for ia, ib in places:
            if (ia, ib) not in self.seen:
                self.seen.add((ia, ib))
                self.mail.await_recv(
                    self.base + 20 + ia * 4 + ib, self.blk(self.owner(ia, ib, True)), self.partner
                )

    def line_out(self, i):
        block = self.blk(self.owner(0, i))
        self.forward(4 + 4 * i, block, self.a_plus)
        self.forward(5 + 4 * i, block, self.a_minus)

    def line_relay(self, i):
        low, high = self.owner(1, i), self.owner(2, i)
        self.mail.await_recv(self.base + 4 + 4 * i, self.blk(low), self.a_minus)
        self.forward(6 + 4 * i, self.blk(low, 0), self.a_plus)
        self.mail.await_recv(self.base + 5 + 4 * i, self.blk(high), self.a_plus)
        self.forward(7 + 4 * i, self.blk(high, 1), self.a_minus)
        self.to_partner(1, i)
        self.to_partner(2, i)

    def line_far(self, i):
        far = self.owner(3, i)
        self.mail.await_recv(self.base + 6 + 4 * i, self.blk(far, 0), self.a_minus)
        self.mail.await_recv(self.base + 7 + 4 * i, self.blk(far, 1), self.a_plus)
        self.to_partner(3, i)

    def stages(self):
        mail, base, blk = self.mail, self.base, self.blk
        own, low, high, far = (self.owner(0, i) for i in range(4))
        self.forward(0, blk(own), self.b_plus)
        self.forward(1, blk(own), self.b_minus)
        self.line_out(0)
        self.to_partner(0, 0)
        mail.await_recv(base + 0, blk(low), self.b_minus)
        self.forward(2, blk(low, 0), self.b_plus)
        self.line_out(1)
        self.to_partner(0, 1)
        mail.await_recv(base + 1, blk(high), self.b_plus)
        self.forward(3, blk(high, 1), self.b_minus)
        self.line_out(2)
        self.to_partner(0, 2)
        self.line_relay(0)
        yield "relay0"
        mail.await_recv(base + 2, blk(far, 0), self.b_minus)
        mail.await_recv(base + 3, blk(far, 1), self.b_plus)
        self.line_out(3)
        self.to_partner(0, 3)
        self.line_relay(1)
        yield "relay1"
        self.line_relay(2)
        yield "relay2"
        self.line_far(0)
        yield "far0"
        self.line_relay(3)
        yield "relay3"
        self.line_far(1)
        yield "far1"
        self.line_far(2)
        yield "far2"
        self.line_far(3)
        yield "far3"

    def finish(self):
        self.from_partner(*[(ia, ib) for ia in range(4) for ib in range(4)])


PIECES = 2
SCATTER_ROLES = 13 * PIECES + 1


def reduce_rows(mail, base, product, width, xs, xr, sums, acc, near, mid, last, swap_out, swap_in):
    x, z, c = place()
    a = (1 - c) * z + c * x
    b = (1 - c) * x + c * z
    partner = moved(0, 0, 1)
    a_plus, a_minus = moved(1, 0), moved(-1, 0)
    b_plus, b_minus, b_far = moved(0, 1), moved(0, -1), moved(0, 2)
    steps = (2, 1, 3, 0)
    f32, bf16 = jnp.float32, jnp.bfloat16
    lo, hi = pl.ds(0, 128), pl.ds(128, 128)

    def set_chips(k, cc):
        return [(1 - cc) * (j * 4 + k) + cc * (k * 4 + j) for j in range(4)]

    def role(p, n):
        return base + 13 * p + n

    def partner_part(p, idx):
        product(set_chips((b + steps[idx]) % 4, 1 - c), 1 - c, p, xs.at[p, idx], None)
        mail.send(role(p, idx), xs.at[p, idx], xr.at[p, idx], partner)

    def own_part(p, idx, out):
        mail.await_recv(role(p, idx), xr.at[p, idx], partner)
        product(set_chips((a + steps[idx]) % 4, c), c, p, out, xr.at[p, idx])

    def far_sets(p):
        partner_part(p, 0)
        partner_part(p, 1)
        own_part(p, 0, sums.at[p, 0])
        mail.send(role(p, 4), sums.at[p, 0, lo], near.at[p, lo], a_plus)
        mail.send(role(p, 5), sums.at[p, 0, hi], near.at[p, hi], a_minus)

    def next_sets(p):
        partner_part(p, 2)
        own_part(p, 1, sums.at[p, 1])
        mail.send(role(p, 6), sums.at[p, 1, hi], mid.at[p, 0, hi], a_plus)
        partner_part(p, 3)
        own_part(p, 2, sums.at[p, 2])
        mail.send(role(p, 7), sums.at[p, 2, lo], mid.at[p, 1, lo], a_minus)

    def pass_on(p):
        mail.await_recv(role(p, 4), near.at[p, lo], a_minus)
        sums[p, 1, lo] = (sums[p, 1, lo].astype(f32) + near[p, lo].astype(f32)).astype(bf16)
        mail.send(role(p, 8), sums.at[p, 1, lo], mid.at[p, 0, lo], a_plus)
        mail.await_recv(role(p, 5), near.at[p, hi], a_plus)
        sums[p, 2, hi] = (sums[p, 2, hi].astype(f32) + near[p, hi].astype(f32)).astype(bf16)
        mail.send(role(p, 9), sums.at[p, 2, hi], mid.at[p, 1, hi], a_minus)

    def own_set(p):
        own_part(p, 3, acc.at[p])

    def chunk(j):
        return pl.ds(pl.multiple_of(j * 64, 64), 64)

    def chunk_sum(p, j):
        at = chunk(j)
        return acc[p, at] + mid[p, 0, at].astype(f32) + mid[p, 1, at].astype(f32)

    def second(p):
        mail.await_recv(role(p, 6), mid.at[p, 0, hi], a_minus)
        mail.await_recv(role(p, 7), mid.at[p, 1, lo], a_plus)
        mail.await_recv(role(p, 8), mid.at[p, 0, lo], a_minus)
        mail.await_recv(role(p, 9), mid.at[p, 1, hi], a_plus)
        for n, (step, to) in enumerate(((2, b_far), (1, b_plus), (3, b_minus))):
            at = chunk((b + step) % 4)
            sums[p, 0, at] = chunk_sum(p, (b + step) % 4).astype(bf16)
            mail.send(role(p, 10 + n), sums.at[p, 0, at], last.at[p, n], to)

    def finish(p):
        value = chunk_sum(p, b)
        for n, source in ((1, b_minus), (2, b_plus), (0, b_far)):
            mail.await_recv(role(p, 10 + n), last.at[p, n], source)
        for n in range(3):
            value = value + last[p, n].astype(f32)
        return value

    far_sets(0)
    next_sets(0)
    far_sets(1)
    pass_on(0)
    next_sets(1)
    own_set(0)
    pass_on(1)
    mail.release(role(0, 4), role(0, 5))
    second(0)
    own_set(1)
    mail.release(role(1, 4), role(1, 5))
    second(1)
    value = jnp.concatenate([finish(0), finish(1)], axis=1)
    is_first = c == 0
    swap_out[...] = jnp.where(is_first, value[32:], value[:32])
    mail.send(base + 13 * PIECES, swap_out, swap_in, partner)
    mine = jnp.where(is_first, value[:32], value[32:])
    mail.await_recv(base + 13 * PIECES, swap_in, partner)
    return mine


TAIL_ROLES = SCATTER_ROLES * 2 + GATHER_ROLES


def tail_kernel(
    heads_ref, w_out_hbm, gain_ref, w_gu_hbm, w_down_hbm, attn_ref, block_ref,
    w_out, w_gu, w_down, load_sems, send_sems, recv_sems,
    xs, xr, sums, acc, near, mid, last, swap_out, swap_in,
    xs2, xr2, sums2, near2, mid2, last2, swap_out2, swap_in2,
    ff_buf, hidden,
):
    x, z, c = place()
    loads = [
        pltpu.make_async_copy(w_out_hbm, w_out, load_sems.at[0]),
        pltpu.make_async_copy(w_gu_hbm, w_gu, load_sems.at[1]),
        pltpu.make_async_copy(w_down_hbm, w_down, load_sems.at[2]),
    ]
    for load in loads:
        load.start()
    greet([
        {"hid": moved(1, 0)}, {"hid": moved(-1, 0)}, {"hid": moved(0, 1)},
        {"hid": moved(0, -1)}, {"hid": moved(0, 2)}, {"hid": moved(0, 0, 1)},
    ])
    mail = Mail(send_sems, recv_sems)
    width = w_out.shape[1] // 2
    step = width // PIECES

    def product_of(lhs, weight):
        def product(chips, half, piece, out, other):
            rows = jnp.concatenate(
                [lhs[pl.ds(pl.multiple_of(chip * 64, 64), 64), :] for chip in chips], axis=0
            )
            cols = pl.ds(pl.multiple_of(half * width + piece * step, 128), step)
            value = jnp.dot(rows, weight[:, cols], preferred_element_type=jnp.float32)
            if other is not None:
                value = value + other[...].astype(jnp.float32)
            out[...] = value.astype(out.dtype)
        return product

    mine_at = pl.ds(pl.multiple_of(c * width, 128), width)
    other_at = pl.ds(pl.multiple_of((1 - c) * width, 128), width)

    loads[0].wait()
    mine = reduce_rows(
        mail, 0, product_of(heads_ref, w_out), width,
        xs, xr, sums, acc, near, mid, last, swap_out, swap_in,
    )
    other = swap_in[...]
    attn_ref[:, mine_at] = mine.astype(jnp.bfloat16)
    attn_ref[:, other_at] = other.astype(jnp.bfloat16)
    total = jnp.sum(mine * mine, axis=1, keepdims=True) + jnp.sum(other * other, axis=1, keepdims=True)
    scale = lax.rsqrt(total / (2 * width) + EPS)
    own_rows = pl.ds(pl.multiple_of(moved(0, 0) * 32, 32), 32)
    gain_mine = gain_ref[mine_at].reshape(1, width)
    gain_other = gain_ref[other_at].reshape(1, width)
    ff_buf[own_rows, mine_at] = (mine * scale * gain_mine).astype(jnp.bfloat16)
    ff_buf[own_rows, other_at] = (other * scale * gain_other).astype(jnp.bfloat16)

    units = w_down.shape[0]
    contract = (((1,), (1,)), ((), ()))
    gather = Gather(mail, SCATTER_ROLES, ff_buf, 32)

    def feed(own, partners):
        gather.from_partner(*partners)
        places = [gather.owner(*at) for at in own] + [gather.owner(*at, True) for at in partners]
        slices = [pl.ds(pl.multiple_of(hid * 32, 32), 32) for hid in places]
        rows = jnp.concatenate([ff_buf[at, :] for at in slices], axis=0)
        gate = lax.dot_general(rows, w_gu[pl.ds(0, units), :], contract, preferred_element_type=jnp.float32)
        up = lax.dot_general(rows, w_gu[pl.ds(units, units), :], contract, preferred_element_type=jnp.float32)
        value = (jax.nn.silu(gate) * up).astype(jnp.bfloat16)
        for n, at in enumerate(slices):
            hidden[at, :] = value[n * 32:(n + 1) * 32]

    for stage in gather.stages():
        if stage == "relay2":
            loads[1].wait()
            feed([(0, 0), (0, 1), (0, 2), (1, 0), (2, 0)], [(0, 0), (0, 1), (0, 2)])
        if stage == "relay3":
            feed([(1, 1), (2, 1), (1, 2), (2, 2), (0, 3), (3, 0)], [(1, 0), (2, 0)])
        if stage == "far3":
            feed([(1, 3), (2, 3)], [(0, 3), (1, 1), (2, 1), (1, 2), (2, 2), (3, 0)])
    feed([(3, 1), (3, 2), (3, 3)], [(1, 3), (2, 3), (3, 1), (3, 2), (3, 3)])

    loads[2].wait()
    mine = reduce_rows(
        mail, SCATTER_ROLES + GATHER_ROLES, product_of(hidden, w_down), width,
        xs2, xr2, sums2, acc, near2, mid2, last2, swap_out2, swap_in2,
    )
    block_ref[:, mine_at] = mine.astype(jnp.bfloat16)
    block_ref[:, other_at] = swap_in2[...].astype(jnp.bfloat16)
    mail.drain()


def tail(heads_out, w_out, gain_ff, w_gu, w_down):
    tok_grp = heads_out.shape[0]
    width = w_out.shape[1]
    half = width // 2
    units = w_down.shape[0]
    bf16, f32 = jnp.bfloat16, jnp.float32
    vmem = pl.BlockSpec(memory_space=pltpu.VMEM)
    anywhere = pl.BlockSpec(memory_space=pl.ANY)

    piece = half // PIECES

    def travel():
        return [
            pltpu.VMEM((PIECES, 4, 256, piece), bf16), pltpu.VMEM((PIECES, 4, 256, piece), bf16),
            pltpu.VMEM((PIECES, 3, 256, piece), bf16),
        ]

    def landing():
        return [
            pltpu.VMEM((PIECES, 256, piece), bf16), pltpu.VMEM((PIECES, 2, 256, piece), bf16),
            pltpu.VMEM((PIECES, 3, 64, piece), bf16), pltpu.VMEM((32, half), f32), pltpu.VMEM((32, half), f32),
        ]

    return pl.pallas_call(
        tail_kernel,
        out_shape=(jax.ShapeDtypeStruct((32, width), bf16), jax.ShapeDtypeStruct((32, width), bf16)),
        in_specs=[vmem, anywhere, vmem, anywhere, anywhere],
        out_specs=(vmem, vmem),
        scratch_shapes=[
            pltpu.VMEM(w_out.shape, bf16), pltpu.VMEM(w_gu.shape, bf16), pltpu.VMEM(w_down.shape, bf16),
            pltpu.SemaphoreType.DMA((3,)), pltpu.SemaphoreType.DMA((TAIL_ROLES,)),
            pltpu.SemaphoreType.DMA((TAIL_ROLES,)),
            *travel(), pltpu.VMEM((PIECES, 256, piece), f32), *landing(),
            *travel(), *landing(),
            pltpu.VMEM((tok_grp, width), bf16), pltpu.VMEM((tok_grp, units), bf16),
        ],
        compiler_params=pltpu.CompilerParams(
            collective_id=0, has_side_effects=True, vmem_limit_bytes=66000000
        ),
        name="tail",
    )(heads_out, w_out, gain_ff, w_gu, w_down)


FRONT_BLOCKS = 36
WINDOW = 768


def front_kernel(
    slot_ref, choice_ref, lengths_ref, tokens_ref, gain_ref, down_hbm, up_ref, w_hbm, cache_hbm, heads_ref,
    w_qkv, w_latent, rows_buf, load_sems, send_sems, recv_sems,
    first_0, first_1, second_0, second_1, pass_0, pass_1, split_0, split_1,
    prefix, qkv, top, denom, total,
):
    x, z, c = place()
    hid = lax.axis_index("hid")
    req = lax.axis_index("req")
    lower, upper = (req + 3) % 4, (req + 1) % 4
    width = tokens_ref.shape[1]
    bf16, f32 = jnp.bfloat16, jnp.float32
    first, second = (first_0, first_1), (second_0, second_1)
    passed, split = (pass_0, pass_1), (split_0, split_1)

    def owner(group):
        return slot_ref[choice_ref[group]]

    peers = [{"hid": (hid + d) % 32} for d in range(1, 32)] + [{"req": lower}, {"req": upper}]
    barrier = pltpu.get_barrier_semaphore()
    for peer in peers:
        pl.semaphore_signal(barrier, inc=1, device_id=peer, device_id_type=MESH)
    latent_load = pltpu.make_async_copy(down_hbm, w_latent, load_sems.at[5])
    latent_load.start()
    loads = []
    for k in range(2):
        for half in range(2):
            copy = pltpu.make_async_copy(
                cache_hbm.at[pl.ds(half * 32 + k * 16, 16)], first[k].at[half], load_sems.at[1 + 2 * k + half]
            )
            copy.start()
            loads.append(copy)
    w_load = pltpu.make_async_copy(w_hbm, w_qkv, load_sems.at[0])
    w_load.start()

    matrix = tokens_ref[...].astype(f32)
    normed = rms_scale(matrix, gain_ref[...].reshape(1, width)).astype(bf16)
    own_rows = pl.ds(pl.multiple_of(hid * 32, 32), 32)
    rows_buf[own_rows, pl.ds(0, width)] = normed
    pl.semaphore_wait(barrier, len(peers))

    mail = Mail(send_sems, recv_sems)
    y_base = GATHER_ROLES
    deal_base = y_base + 8

    def y_copy(role, src, dst, to):
        return pltpu.make_async_remote_copy(
            src_ref=src, dst_ref=dst, send_sem=send_sems.at[role], recv_sem=recv_sems.at[role],
            device_id={"req": to}, device_id_type=MESH,
        )

    def y_send(role, src, dst, to):
        copy = y_copy(role, src, dst, to)
        copy.start()
        mail.sent[role] = copy

    def y_start():
        for k in range(2):
            y_send(y_base + k, cache_hbm.at[pl.ds(k * 16, 16)], first[k].at[2], lower)
            y_send(y_base + 2 + k, cache_hbm.at[pl.ds(32 + k * 16, 16)], first[k].at[3], upper)

    def y_pass(k):
        loads[2 * k].wait()
        loads[2 * k + 1].wait()
        y_copy(y_base + k, first[k].at[2], first[k].at[2], upper).wait_recv()
        y_copy(y_base + 2 + k, first[k].at[3], first[k].at[3], lower).wait_recv()
        passed[k][0] = first[k][jnp.where(owner(lower) == req, 1, 2)]
        y_send(y_base + 4 + k, passed[k].at[0], second[k].at[0], lower)
        passed[k][1] = first[k][jnp.where(owner(upper) == req, 0, 3)]
        y_send(y_base + 6 + k, passed[k].at[1], second[k].at[1], upper)

    def deal(k):
        y_copy(y_base + 4 + k, second[k].at[0], second[k].at[0], upper).wait_recv()
        y_copy(y_base + 6 + k, second[k].at[1], second[k].at[1], lower).wait_recv()
        away = (owner(req) - req + 4) % 4
        late_a = jnp.full((1, 1, 1), (away >= 2).astype(jnp.int32)) > 0
        late_b = jnp.full((1, 1, 1), jnp.logical_or(away == 1, away == 2).astype(jnp.int32)) > 0
        half_a = jnp.where(late_a, second[k][jnp.where(away == 2, 0, 1)], first[k][jnp.where(away == 0, 0, 2)])
        half_b = jnp.where(late_b, second[k][jnp.where(away == 1, 0, 1)], first[k][jnp.where(away == 0, 1, 3)])
        r = lax.broadcasted_iota(jnp.int32, (32, 32), 0)
        s = lax.broadcasted_iota(jnp.int32, (32, 32), 1)
        sort = (s == jnp.where(r < 16, 2 * r, 2 * r - 31)).astype(bf16)
        zeros = jnp.zeros((16, 256 - HD), bf16)
        for half, value in enumerate((half_a, half_b)):
            planes = jnp.dot(sort, value.reshape(32, width), preferred_element_type=f32).astype(bf16)
            for kv in range(2):
                for h in range(32):
                    piece = planes[kv * 16:(kv + 1) * 16, h * HD:(h + 1) * HD]
                    split[k][h, kv, pl.ds(half * 16, 16), :] = jnp.concatenate([piece, zeros], axis=1)

        landing = prefix.at[k, :, own_rows]
        for d in range(1, 32):
            to = (hid + d) % 32
            mail.send(deal_base + k * 31 + d - 1, split[k].at[to], landing, to)
        prefix[k, :, own_rows] = split[k][hid]

    def dealt(k):
        for d in range(1, 32):
            source = (hid + 32 - d) % 32
            landing = prefix.at[k, :, pl.ds(pl.multiple_of(source * 32, 32), 32)]
            mail.await_recv(deal_base + k * 31 + d - 1, landing, source)

    y_start()
    latent_load.wait()
    latent = jnp.dot(normed, w_latent[...], preferred_element_type=f32)
    rows_buf[own_rows, pl.ds(width, 128)] = latent.astype(bf16)
    gather = Gather(mail, 0, rows_buf, 32)
    for stage in gather.stages():
        if stage == "relay0":
            y_pass(0)
        if stage == "relay2":
            y_pass(1)
        if stage == "relay3":
            deal(0)
    deal(1)
    gather.finish()

    w_load.wait()
    contract = (((1,), (1,)), ((), ()))
    pad = jnp.zeros((256, 256 - HD), bf16)

    @pl.loop(0, 4)
    def _(i):
        at = pl.ds(pl.multiple_of(i * 256, 256), 256)
        rows = rows_buf[at, pl.ds(0, width)]
        for part in range(3):
            value = lax.dot_general(
                rows, w_qkv[pl.ds(part * HD, HD), :], contract, preferred_element_type=f32
            )
            if part == 0:
                value = value + lax.dot_general(
                    rows_buf[at, pl.ds(width, 128)], up_ref[...], contract, preferred_element_type=f32
                )
            qkv[part, at, :] = jnp.concatenate([value.astype(bf16), pad], axis=1)

    dealt(0)

    ends = [lengths_ref[0, 0]]
    for n in range(1, lengths_ref.shape[1]):
        ends.append(ends[-1] + lengths_ref[0, n])
    factor = HD ** (-0.5)

    @pl.loop(0, 8)
    def _(i):
        at = pl.ds(pl.multiple_of(i * 128, 128), 128)
        begin = jnp.minimum(jnp.maximum(i * 128 - 512, 0), 1024 - WINDOW)
        near = pl.ds(pl.multiple_of(begin, 128), WINDOW)
        q = qkv[0, at, :]
        s_far = lax.dot_general(q, prefix[0, 0], contract, preferred_element_type=f32) * factor
        s_near = lax.dot_general(q, qkv[1, near, :], contract, preferred_element_type=f32) * factor
        row = lax.broadcasted_iota(jnp.int32, (128, 1), 0) + i * 128
        since = jnp.zeros((128, 1), jnp.int32)
        for end in ends:
            since = jnp.where(row >= end, jnp.maximum(since, end), since)
        col = lax.broadcasted_iota(jnp.int32, (128, WINDOW), 1) + begin
        s_near = jnp.where(jnp.logical_and(col >= since, col <= row), s_near, -jnp.inf)
        row_max = jnp.maximum(
            jnp.max(s_far, axis=1, keepdims=True), jnp.max(s_near, axis=1, keepdims=True)
        )
        e_far = jnp.exp(s_far - row_max)
        e_near = jnp.exp(s_near - row_max)
        top[at, :] = row_max
        denom[at, :] = jnp.sum(e_far, axis=1, keepdims=True) + jnp.sum(e_near, axis=1, keepdims=True)
        out = jnp.dot(e_far.astype(bf16), prefix[0, 1], preferred_element_type=f32)
        total[at, :] = out + jnp.dot(e_near.astype(bf16), qkv[2, near, :], preferred_element_type=f32)

    dealt(1)

    @pl.loop(0, 8)
    def _(i):
        at = pl.ds(pl.multiple_of(i * 128, 128), 128)
        scores = lax.dot_general(qkv[0, at, :], prefix[1, 0], contract, preferred_element_type=f32) * factor
        row_max = jnp.maximum(top[at, :], jnp.max(scores, axis=1, keepdims=True))
        keep = jnp.exp(top[at, :] - row_max)
        expos = jnp.exp(scores - row_max)
        row_sum = denom[at, :] * keep + jnp.sum(expos, axis=1, keepdims=True)
        out = total[at, :] * keep + jnp.dot(expos.astype(bf16), prefix[1, 1], preferred_element_type=f32)
        heads_ref[at, :] = (out / row_sum)[:, :HD].astype(bf16)

    mail.drain()


def front(slots, choices, lengths, tokens, gain_in, adapt_down, up_t, w_t, cache):
    rows, width = tokens.shape
    tok_grp = rows * 32
    bf16 = jnp.bfloat16
    smem = pl.BlockSpec(memory_space=pltpu.SMEM)
    vmem = pl.BlockSpec(memory_space=pltpu.VMEM)
    anywhere = pl.BlockSpec(memory_space=pl.ANY)
    roles = GATHER_ROLES + 8 + 62

    def halves(count):
        return pltpu.VMEM((count, 16, 2, width), bf16)

    return pl.pallas_call(
        front_kernel,
        out_shape=jax.ShapeDtypeStruct((tok_grp, HD), bf16),
        in_specs=[smem, smem, smem, vmem, vmem, anywhere, vmem, anywhere, anywhere],
        out_specs=vmem,
        scratch_shapes=[
            pltpu.VMEM(w_t.shape, bf16), pltpu.VMEM(adapt_down.shape, bf16),
            pltpu.VMEM((tok_grp, width + 128), bf16),
            pltpu.SemaphoreType.DMA((6,)), pltpu.SemaphoreType.DMA((roles,)),
            pltpu.SemaphoreType.DMA((roles,)),
            halves(4), halves(4), halves(2), halves(2), halves(2), halves(2),
            pltpu.VMEM((32, 2, 32, 256), bf16), pltpu.VMEM((32, 2, 32, 256), bf16),
            pltpu.VMEM((2, 2, tok_grp, 256), bf16), pltpu.VMEM((3, tok_grp, 256), bf16),
            pltpu.VMEM((tok_grp, 1), jnp.float32), pltpu.VMEM((tok_grp, 1), jnp.float32),
            pltpu.VMEM((tok_grp, 256), jnp.float32),
        ],
        compiler_params=pltpu.CompilerParams(
            collective_id=1, has_side_effects=True, vmem_limit_bytes=66000000
        ),
        name="front",
    )(slots, choices, lengths, tokens, gain_in, adapt_down, up_t, w_t, cache)


def settle_kernel(attn_ref, block_ref, attn_out, block_out):
    attn_out[...] = attn_ref[...]
    block_out[...] = block_ref[...]


def settle(attn, block):
    vmem = pl.BlockSpec(memory_space=pltpu.VMEM)
    return pl.pallas_call(
        settle_kernel,
        out_shape=(jax.ShapeDtypeStruct(attn.shape, attn.dtype), jax.ShapeDtypeStruct(block.shape, block.dtype)),
        in_specs=[vmem, vmem],
        out_specs=(vmem, vmem),
        name="settle",
    )(attn, block)


def per_device(
    tokens,
    gain_in,
    w_qkv,
    adapt_down,
    adapt_up,
    w_out,
    gain_ff,
    w_gate_up,
    w_down,
    prefix_cache,
    prefix_owner,
    group_prefix,
    lengths,
):
    w_t = jnp.transpose(w_qkv, (1, 2, 0)).reshape(3 * w_qkv.shape[2], w_qkv.shape[0])
    w_gu = jnp.transpose(w_gate_up, (1, 2, 0)).reshape(2 * w_gate_up.shape[2], w_gate_up.shape[0])
    heads_out = front(
        prefix_owner, group_prefix, lengths, tokens, gain_in, adapt_down, adapt_up.T, w_t, prefix_cache[0]
    )
    return settle(*tail(heads_out, w_out, gain_ff, w_gu, w_down))


def solution(mesh):
    placed = (
        P(("req", "hid"), None),
        P(),
        P(None, None, "hid"),
        P(),
        P(None, "hid"),
        P("hid", None),
        P(),
        P(None, None, "hid"),
        P("hid", None),
        P("req", "hid", None, None),
        P(),
        P(),
        P("req", None),
    )
    return jax.shard_map(
        per_device,
        mesh=mesh,
        in_specs=placed,
        out_specs=(P(("req", "hid"), None), P(("req", "hid"), None)),
        check_vma=False,
    )
```

time: 209 us -> 194 us (0.928)
  Pallas kernels: 202 us -> 193 us
  local copies, waits for them, and re-layouts: 5.76 us -> 0 us
    pallas_call x1, Pallas kernels: 101 us -> 89.4 us  [front(): pl.pallas_call(front_kernel, out_shape=jax.ShapeDtypeStruct((tok_grp, HD)...]
    unnamed x4 -> x0, local copies, waits for them, and re-layouts: 3.29 us -> none
where the time goes in v3:
time: 194 us
  Pallas kernels  193 us (99%)
    pallas_call x1, Pallas kernels, tail(): pl.pallas_call(tail_kernel, out_shape=(jax.ShapeDtypeStruct((32, width),...  102 us
    pallas_call x1, Pallas kernels, front(): pl.pallas_call(front_kernel, out_shape=jax.ShapeDtypeStruct((tok_grp, HD)...  89.4 us

profile of v3, /device:TPU:1, one launch (start us, length us, event | category | flops | bytes accessed | tf_op | source)
XLA Modules:
  0.0 193.6 jit_solution(649929064592191954)
XLA Ops:
  0.6 89.4 %front.1.heads_ref = bf16[1024,224]{1,0:T(8,128)(2,1)} custom-call(s32[3]{0:T(128)} %slot_ref.1, s32[4]{0:T(128)} %choice_ref.1, s32[1,6]{1,0:T(1,128)} %lengths_ref.1, bf16[32,7168]{1,0:T(8,128)(2,1)} %tokens_ref.1, f32[7168]{0:T(1024)} %gain_ref.2, bf16[7168,128]{1,0:T(8,128)(2,1)} %down_hbm.1, bf16[224,128]{1,0:T(8,128)(2,1)} %bitcast.11, ...), custom_call_target="tpu_custom_call" | custom-call | tf_op jit(solution)/shard_map/front/pallas_call | solution.py:602
  90.1 101.7 %tail.1 = (bf16[32,3584]{1,0:T(8,128)(2,1)}, bf16[32,3584]{1,0:T(8,128)(2,1)}) custom-call(bf16[1024,224]{1,0:T(8,128)(2,1)} %front.1.heads_ref, bf16[224,3584]{1,0:T(8,128)(2,1)} %w_out_hbm.1, f32[3584]{0:T(1024)} %gain_ref.3, bf16[896,3584]{1,0:T(8,128)(2,1)} %bitcast.9, bf16[448,3584]{1,0:T(8,128)(2,1)} %w_down_hbm.1), custom_call_target="tpu_custom_call" | custom-call | tf_op jit(solution)/shard_map/tail/pallas_call | solution.py:384
  191.8 1.8 settle.1

commit v4 on v3

--- a/solution.py
+++ b/solution.py
@@ -39,13 +39,6 @@
     )
 
 
-def greet(peers):
-    barrier = pltpu.get_barrier_semaphore()
-    for peer in peers:
-        pl.semaphore_signal(barrier, inc=1, device_id=peer, device_id_type=MESH)
-    pl.semaphore_wait(barrier, len(peers))
-
-
 class Mail:
     def __init__(self, send_sems, recv_sems):
         self.send_sems, self.recv_sems, self.sent = send_sems, recv_sems, {}
@@ -55,10 +48,6 @@
         copy.start()
         self.sent[role] = copy
 
-    def release(self, *roles):
-        for role in roles:
-            self.sent.pop(role).wait_send()
-
     def await_recv(self, role, dst, hid):
         remote(dst, dst, self.send_sems.at[role], self.recv_sems.at[role], hid).wait_recv()
 
@@ -72,17 +61,24 @@
 
 
 class Gather:
-    def __init__(self, mail, base, buf, rows):
+    def __init__(self, mail, base, buf, rows, first_row=0, split_columns=False):
         self.mail, self.base, self.buf, self.rows = mail, base, buf, rows
+        self.first_row, self.split_columns = first_row, split_columns
         self.a_plus, self.a_minus = moved(1, 0), moved(-1, 0)
         self.b_plus, self.b_minus = moved(0, 1), moved(0, -1)
         self.partner = moved(0, 0, 1)
         self.seen = set()
 
+    def row_slice(self, hid):
+        return pl.ds(pl.multiple_of(self.first_row + hid * self.rows, self.rows), self.rows)
+
     def blk(self, hid, part=None):
-        start = pl.multiple_of(hid * self.rows, self.rows)
+        start = pl.multiple_of(self.first_row + hid * self.rows, self.rows)
         if part is None:
-            return self.buf.at[pl.ds(start, self.rows)]
+            return self.buf.at[self.row_slice(hid)]
+        if self.split_columns:
+            half = self.buf.shape[1] // 2
+            return self.buf.at[self.row_slice(hid), pl.ds(part * half, half)]
         half = self.rows // 2
         return self.buf.at[pl.ds(start + part * half, half)]
 
@@ -132,6 +128,7 @@
         self.forward(1, blk(own), self.b_minus)
         self.line_out(0)
         self.to_partner(0, 0)
+        yield "start"
         mail.await_recv(base + 0, blk(low), self.b_minus)
         self.forward(2, blk(low, 0), self.b_plus)
         self.line_out(1)
@@ -166,195 +163,240 @@
 
 
 PIECES = 2
-SCATTER_ROLES = 13 * PIECES + 1
-
-
-def reduce_rows(mail, base, product, width, xs, xr, sums, acc, near, mid, last, swap_out, swap_in):
-    x, z, c = place()
-    a = (1 - c) * z + c * x
-    b = (1 - c) * x + c * z
-    partner = moved(0, 0, 1)
-    a_plus, a_minus = moved(1, 0), moved(-1, 0)
-    b_plus, b_minus, b_far = moved(0, 1), moved(0, -1), moved(0, 2)
-    steps = (2, 1, 3, 0)
-    f32, bf16 = jnp.float32, jnp.bfloat16
-    lo, hi = pl.ds(0, 128), pl.ds(128, 128)
-
-    def set_chips(k, cc):
+PART = 16
+PIECE_ROLES = 14
+
+
+class Scatter:
+    def __init__(self, mail, base, product, xs, xr, sums, acc, near, mid, last, swap_out, swap_in):
+        self.mail, self.base, self.product = mail, base, product
+        self.xs, self.xr, self.sums, self.acc = xs, xr, sums, acc
+        self.near, self.mid, self.last = near, mid, last
+        self.swap_out, self.swap_in = swap_out, swap_in
+        x, z, c = place()
+        self.c = c
+        self.a = (1 - c) * z + c * x
+        self.b = (1 - c) * x + c * z
+        self.partner = moved(0, 0, 1)
+        self.a_plus, self.a_minus = moved(1, 0), moved(-1, 0)
+        self.b_plus, self.b_minus, self.b_far = moved(0, 1), moved(0, -1), moved(0, 2)
+        self.lo, self.hi = pl.ds(0, 4 * PART), pl.ds(4 * PART, 4 * PART)
+
+    def role(self, p, n):
+        return self.base + PIECE_ROLES * p + n
+
+    def set_chips(self, k, cc):
         return [(1 - cc) * (j * 4 + k) + cc * (k * 4 + j) for j in range(4)]
 
-    def role(p, n):
-        return base + 13 * p + n
-
-    def partner_part(p, idx):
-        product(set_chips((b + steps[idx]) % 4, 1 - c), 1 - c, p, xs.at[p, idx], None)
-        mail.send(role(p, idx), xs.at[p, idx], xr.at[p, idx], partner)
-
-    def own_part(p, idx, out):
-        mail.await_recv(role(p, idx), xr.at[p, idx], partner)
-        product(set_chips((a + steps[idx]) % 4, c), c, p, out, xr.at[p, idx])
-
-    def far_sets(p):
-        partner_part(p, 0)
-        partner_part(p, 1)
-        own_part(p, 0, sums.at[p, 0])
-        mail.send(role(p, 4), sums.at[p, 0, lo], near.at[p, lo], a_plus)
-        mail.send(role(p, 5), sums.at[p, 0, hi], near.at[p, hi], a_minus)
-
-    def next_sets(p):
-        partner_part(p, 2)
-        own_part(p, 1, sums.at[p, 1])
-        mail.send(role(p, 6), sums.at[p, 1, hi], mid.at[p, 0, hi], a_plus)
-        partner_part(p, 3)
-        own_part(p, 2, sums.at[p, 2])
-        mail.send(role(p, 7), sums.at[p, 2, lo], mid.at[p, 1, lo], a_minus)
-
-    def pass_on(p):
-        mail.await_recv(role(p, 4), near.at[p, lo], a_minus)
+    def partner_part(self, p, idx):
+        c, step = self.c, (2, 1, 3, 0)[idx]
+        chips = self.set_chips((self.b + step) % 4, 1 - c)
+        self.product(chips, 1 - c, p, self.xs.at[p, idx], None)
+        self.mail.send(self.role(p, idx), self.xs.at[p, idx], self.xr.at[p, idx], self.partner)
+
+    def own_part(self, p, idx, out):
+        c, step = self.c, (2, 1, 3, 0)[idx]
+        self.mail.await_recv(self.role(p, idx), self.xr.at[p, idx], self.partner)
+        self.product(self.set_chips((self.a + step) % 4, c), c, p, out, self.xr.at[p, idx])
+
+    def far_sets(self, p):
+        sums, near = self.sums, self.near
+        self.partner_part(p, 0)
+        self.partner_part(p, 1)
+        self.own_part(p, 0, sums.at[p, 0])
+        self.mail.send(self.role(p, 4), sums.at[p, 0, self.lo], near.at[p, self.lo], self.a_plus)
+        self.mail.send(self.role(p, 5), sums.at[p, 0, self.hi], near.at[p, self.hi], self.a_minus)
+
+    def next_sets(self, p):
+        sums, mid = self.sums, self.mid
+        self.partner_part(p, 2)
+        self.own_part(p, 1, sums.at[p, 1])
+        self.mail.send(self.role(p, 6), sums.at[p, 1, self.hi], mid.at[p, 0, self.hi], self.a_plus)
+        self.partner_part(p, 3)
+        self.own_part(p, 2, sums.at[p, 2])
+        self.mail.send(self.role(p, 7), sums.at[p, 2, self.lo], mid.at[p, 1, self.lo], self.a_minus)
+
+    def pass_on(self, p):
+        f32, bf16 = jnp.float32, jnp.bfloat16
+        sums, near, mid, lo, hi = self.sums, self.near, self.mid, self.lo, self.hi
+        self.mail.await_recv(self.role(p, 4), near.at[p, lo], self.a_minus)
         sums[p, 1, lo] = (sums[p, 1, lo].astype(f32) + near[p, lo].astype(f32)).astype(bf16)
-        mail.send(role(p, 8), sums.at[p, 1, lo], mid.at[p, 0, lo], a_plus)
-        mail.await_recv(role(p, 5), near.at[p, hi], a_plus)
+        self.mail.send(self.role(p, 8), sums.at[p, 1, lo], mid.at[p, 0, lo], self.a_plus)
+        self.mail.await_recv(self.role(p, 5), near.at[p, hi], self.a_plus)
         sums[p, 2, hi] = (sums[p, 2, hi].astype(f32) + near[p, hi].astype(f32)).astype(bf16)
-        mail.send(role(p, 9), sums.at[p, 2, hi], mid.at[p, 1, hi], a_minus)
-
-    def own_set(p):
-        own_part(p, 3, acc.at[p])
-
-    def chunk(j):
-        return pl.ds(pl.multiple_of(j * 64, 64), 64)
-
-    def chunk_sum(p, j):
-        at = chunk(j)
-        return acc[p, at] + mid[p, 0, at].astype(f32) + mid[p, 1, at].astype(f32)
-
-    def second(p):
-        mail.await_recv(role(p, 6), mid.at[p, 0, hi], a_minus)
-        mail.await_recv(role(p, 7), mid.at[p, 1, lo], a_plus)
-        mail.await_recv(role(p, 8), mid.at[p, 0, lo], a_minus)
-        mail.await_recv(role(p, 9), mid.at[p, 1, hi], a_plus)
-        for n, (step, to) in enumerate(((2, b_far), (1, b_plus), (3, b_minus))):
-            at = chunk((b + step) % 4)
-            sums[p, 0, at] = chunk_sum(p, (b + step) % 4).astype(bf16)
-            mail.send(role(p, 10 + n), sums.at[p, 0, at], last.at[p, n], to)
-
-    def finish(p):
-        value = chunk_sum(p, b)
-        for n, source in ((1, b_minus), (2, b_plus), (0, b_far)):
-            mail.await_recv(role(p, 10 + n), last.at[p, n], source)
+        self.mail.send(self.role(p, 9), sums.at[p, 2, hi], mid.at[p, 1, hi], self.a_minus)
+
+    def own_set(self, p):
+        self.own_part(p, 3, self.acc.at[p])
+
+    def chunk(self, j):
+        return pl.ds(pl.multiple_of(j * 2 * PART, 2 * PART), 2 * PART)
+
+    def chunk_sum(self, p, j):
+        at = self.chunk(j)
+        value = self.acc[p, at] + self.mid[p, 0, at].astype(jnp.float32)
+        return value + self.mid[p, 1, at].astype(jnp.float32)
+
+    def second(self, p):
+        mid, q = self.mid, self.sums
+        self.mail.await_recv(self.role(p, 6), mid.at[p, 0, self.hi], self.a_minus)
+        self.mail.await_recv(self.role(p, 7), mid.at[p, 1, self.lo], self.a_plus)
+        self.mail.await_recv(self.role(p, 8), mid.at[p, 0, self.lo], self.a_minus)
+        self.mail.await_recv(self.role(p, 9), mid.at[p, 1, self.hi], self.a_plus)
+        for n, (step, to) in enumerate(((2, self.b_far), (1, self.b_plus), (3, self.b_minus))):
+            j = (self.b + step) % 4
+            q[p, 3, self.chunk(j)] = self.chunk_sum(p, j).astype(jnp.bfloat16)
+            self.mail.send(self.role(p, 10 + n), q.at[p, 3, self.chunk(j)], self.last.at[p, n], to)
+
+    def settle(self, p):
+        value = self.chunk_sum(p, self.b)
+        for n, source in ((1, self.b_minus), (2, self.b_plus), (0, self.b_far)):
+            self.mail.await_recv(self.role(p, 10 + n), self.last.at[p, n], source)
         for n in range(3):
-            value = value + last[p, n].astype(f32)
-        return value
-
-    far_sets(0)
-    next_sets(0)
-    far_sets(1)
-    pass_on(0)
-    next_sets(1)
-    own_set(0)
-    pass_on(1)
-    mail.release(role(0, 4), role(0, 5))
-    second(0)
-    own_set(1)
-    mail.release(role(1, 4), role(1, 5))
-    second(1)
-    value = jnp.concatenate([finish(0), finish(1)], axis=1)
-    is_first = c == 0
-    swap_out[...] = jnp.where(is_first, value[32:], value[:32])
-    mail.send(base + 13 * PIECES, swap_out, swap_in, partner)
-    mine = jnp.where(is_first, value[:32], value[32:])
-    mail.await_recv(base + 13 * PIECES, swap_in, partner)
-    return mine
-
-
-TAIL_ROLES = SCATTER_ROLES * 2 + GATHER_ROLES
+            value = value + self.last[p, n].astype(jnp.float32)
+        is_first = self.c == 0
+        self.swap_out[p] = jnp.where(is_first, value[PART:], value[:PART])
+        self.mail.send(self.role(p, 13), self.swap_out.at[p], self.swap_in.at[p], self.partner)
+        return jnp.where(is_first, value[:PART], value[PART:])
+
+    def other(self, p):
+        self.mail.await_recv(self.role(p, 13), self.swap_in.at[p], self.partner)
+        return self.swap_in[p]
+
+
+TAIL_ROLES = PIECE_ROLES * PIECES * 2 + GATHER_ROLES * PIECES
 
 
 def tail_kernel(
     heads_ref, w_out_hbm, gain_ref, w_gu_hbm, w_down_hbm, attn_ref, block_ref,
-    w_out, w_gu, w_down, load_sems, send_sems, recv_sems,
-    xs, xr, sums, acc, near, mid, last, swap_out, swap_in,
-    xs2, xr2, sums2, near2, mid2, last2, swap_out2, swap_in2,
-    ff_buf, hidden,
+    w_out, w_gu, w_down, load_sems, send_sems, recv_sems, *scratch,
 ):
+    *scatter_refs, ff_buf, hidden = scratch
     x, z, c = place()
     loads = [
         pltpu.make_async_copy(w_out_hbm, w_out, load_sems.at[0]),
         pltpu.make_async_copy(w_gu_hbm, w_gu, load_sems.at[1]),
         pltpu.make_async_copy(w_down_hbm, w_down, load_sems.at[2]),
     ]
+    peers = [
+        {"hid": moved(1, 0)}, {"hid": moved(-1, 0)}, {"hid": moved(0, 1)},
+        {"hid": moved(0, -1)}, {"hid": moved(0, 2)}, {"hid": moved(0, 0, 1)},
+    ]
+    barrier = pltpu.get_barrier_semaphore()
+    for peer in peers:
+        pl.semaphore_signal(barrier, inc=1, device_id=peer, device_id_type=MESH)
     for load in loads:
         load.start()
-    greet([
-        {"hid": moved(1, 0)}, {"hid": moved(-1, 0)}, {"hid": moved(0, 1)},
-        {"hid": moved(0, -1)}, {"hid": moved(0, 2)}, {"hid": moved(0, 0, 1)},
-    ])
+    pl.semaphore_wait(barrier, len(peers))
     mail = Mail(send_sems, recv_sems)
     width = w_out.shape[1] // 2
-    step = width // PIECES
-
-    def product_of(lhs, weight):
-        def product(chips, half, piece, out, other):
-            rows = jnp.concatenate(
-                [lhs[pl.ds(pl.multiple_of(chip * 64, 64), 64), :] for chip in chips], axis=0
-            )
-            cols = pl.ds(pl.multiple_of(half * width + piece * step, 128), step)
+    units = w_down.shape[0]
+    count = heads_ref.shape[0] // PIECES
+
+    def product_of(lhs_rows, weight):
+        def product(chips, half, p, out, other):
+            rows = jnp.concatenate([r for chip in chips for r in lhs_rows(p, chip)], axis=0)
+            cols = pl.ds(pl.multiple_of(half * width, 128), width)
             value = jnp.dot(rows, weight[:, cols], preferred_element_type=jnp.float32)
             if other is not None:
                 value = value + other[...].astype(jnp.float32)
             out[...] = value.astype(out.dtype)
         return product
 
+    def heads_rows(p, chip):
+        return [
+            heads_ref[pl.ds(pl.multiple_of(chip * 64 + core * 32 + p * PART, PART), PART), :]
+            for core in range(2)
+        ]
+
+    def hidden_rows(p, chip):
+        return [hidden[pl.ds(pl.multiple_of(p * count + chip * 2 * PART, 2 * PART), 2 * PART), :]]
+
+    outer = Scatter(mail, 0, product_of(heads_rows, w_out), *scatter_refs[:9])
+    gathers = [
+        Gather(
+            mail, PIECE_ROLES * PIECES + GATHER_ROLES * p, ff_buf, PART,
+            first_row=p * count, split_columns=True,
+        )
+        for p in range(PIECES)
+    ]
+    inner = Scatter(
+        mail, PIECE_ROLES * PIECES + GATHER_ROLES * PIECES, product_of(hidden_rows, w_down), *scatter_refs[9:]
+    )
     mine_at = pl.ds(pl.multiple_of(c * width, 128), width)
     other_at = pl.ds(pl.multiple_of((1 - c) * width, 128), width)
-
-    loads[0].wait()
-    mine = reduce_rows(
-        mail, 0, product_of(heads_ref, w_out), width,
-        xs, xr, sums, acc, near, mid, last, swap_out, swap_in,
-    )
-    other = swap_in[...]
-    attn_ref[:, mine_at] = mine.astype(jnp.bfloat16)
-    attn_ref[:, other_at] = other.astype(jnp.bfloat16)
-    total = jnp.sum(mine * mine, axis=1, keepdims=True) + jnp.sum(other * other, axis=1, keepdims=True)
-    scale = lax.rsqrt(total / (2 * width) + EPS)
-    own_rows = pl.ds(pl.multiple_of(moved(0, 0) * 32, 32), 32)
     gain_mine = gain_ref[mine_at].reshape(1, width)
     gain_other = gain_ref[other_at].reshape(1, width)
-    ff_buf[own_rows, mine_at] = (mine * scale * gain_mine).astype(jnp.bfloat16)
-    ff_buf[own_rows, other_at] = (other * scale * gain_other).astype(jnp.bfloat16)
-
-    units = w_down.shape[0]
-    contract = (((1,), (1,)), ((), ()))
-    gather = Gather(mail, SCATTER_ROLES, ff_buf, 32)
-
-    def feed(own, partners):
-        gather.from_partner(*partners)
-        places = [gather.owner(*at) for at in own] + [gather.owner(*at, True) for at in partners]
-        slices = [pl.ds(pl.multiple_of(hid * 32, 32), 32) for hid in places]
-        rows = jnp.concatenate([ff_buf[at, :] for at in slices], axis=0)
+
+    def normalise(p, mine):
+        other = outer.other(p)
+        rows = pl.ds(p * PART, PART)
+        attn_ref[rows, mine_at] = mine.astype(jnp.bfloat16)
+        attn_ref[rows, other_at] = other.astype(jnp.bfloat16)
+        total = jnp.sum(mine * mine, axis=1, keepdims=True) + jnp.sum(other * other, axis=1, keepdims=True)
+        scale = lax.rsqrt(total / (2 * width) + EPS)
+        own_rows = gathers[p].row_slice(moved(0, 0))
+        ff_buf[own_rows, mine_at] = (mine * scale * gain_mine).astype(jnp.bfloat16)
+        ff_buf[own_rows, other_at] = (other * scale * gain_other).astype(jnp.bfloat16)
+
+    def feed(p, part):
+        contract = (((1,), (1,)), ((), ()))
+        at = pl.ds(p * count + part * (count // 2), count // 2)
+        rows = ff_buf[at, :]
         gate = lax.dot_general(rows, w_gu[pl.ds(0, units), :], contract, preferred_element_type=jnp.float32)
         up = lax.dot_general(rows, w_gu[pl.ds(units, units), :], contract, preferred_element_type=jnp.float32)
-        value = (jax.nn.silu(gate) * up).astype(jnp.bfloat16)
-        for n, at in enumerate(slices):
-            hidden[at, :] = value[n * 32:(n + 1) * 32]
-
-    for stage in gather.stages():
-        if stage == "relay2":
-            loads[1].wait()
-            feed([(0, 0), (0, 1), (0, 2), (1, 0), (2, 0)], [(0, 0), (0, 1), (0, 2)])
-        if stage == "relay3":
-            feed([(1, 1), (2, 1), (1, 2), (2, 2), (0, 3), (3, 0)], [(1, 0), (2, 0)])
-        if stage == "far3":
-            feed([(1, 3), (2, 3)], [(0, 3), (1, 1), (2, 1), (1, 2), (2, 2), (3, 0)])
-    feed([(3, 1), (3, 2), (3, 3)], [(1, 3), (2, 3), (3, 1), (3, 2), (3, 3)])
-
+        hidden[at, :] = (jax.nn.silu(gate) * up).astype(jnp.bfloat16)
+
+    loads[0].wait()
+    outer.far_sets(0)
+    outer.next_sets(0)
+    outer.far_sets(1)
+    outer.pass_on(0)
+    outer.next_sets(1)
+    outer.own_set(0)
+    outer.second(0)
+    outer.pass_on(1)
+    outer.own_set(1)
+    first = outer.settle(0)
+    outer.second(1)
+    stages = [gather.stages() for gather in gathers]
+    normalise(0, first)
+    next(stages[0])
+    second = outer.settle(1)
+    normalise(1, second)
+    next(stages[1])
+    for name in ("relay0", "relay1", "relay2", "far0", "relay3"):
+        for stage in stages:
+            assert next(stage) == name
+    for name in ("far1", "far2", "far3"):
+        next(stages[0])
+    loads[1].wait()
+    gathers[0].finish()
+    feed(0, 0)
+    for name in ("far1", "far2", "far3"):
+        next(stages[1])
+    feed(0, 1)
     loads[2].wait()
-    mine = reduce_rows(
-        mail, SCATTER_ROLES + GATHER_ROLES, product_of(hidden, w_down), width,
-        xs2, xr2, sums2, acc, near2, mid2, last2, swap_out2, swap_in2,
-    )
-    block_ref[:, mine_at] = mine.astype(jnp.bfloat16)
-    block_ref[:, other_at] = swap_in2[...].astype(jnp.bfloat16)
+    inner.far_sets(0)
+    inner.next_sets(0)
+    gathers[1].finish()
+    feed(1, 0)
+    inner.pass_on(0)
+    feed(1, 1)
+    inner.far_sets(1)
+    inner.next_sets(1)
+    inner.own_set(0)
+    inner.second(0)
+    inner.pass_on(1)
+    inner.own_set(1)
+    first = inner.settle(0)
+    inner.second(1)
+    for p, mine in enumerate((first, None)):
+        if mine is None:
+            mine = inner.settle(p)
+        rows = pl.ds(p * PART, PART)
+        block_ref[rows, mine_at] = mine.astype(jnp.bfloat16)
+        block_ref[rows, other_at] = inner.other(p).astype(jnp.bfloat16)
     mail.drain()
 
 
@@ -367,18 +409,15 @@
     vmem = pl.BlockSpec(memory_space=pltpu.VMEM)
     anywhere = pl.BlockSpec(memory_space=pl.ANY)
 
-    piece = half // PIECES
-
-    def travel():
+    set_rows = 8 * PART
+
+    def scatter_scratch():
         return [
-            pltpu.VMEM((PIECES, 4, 256, piece), bf16), pltpu.VMEM((PIECES, 4, 256, piece), bf16),
-            pltpu.VMEM((PIECES, 3, 256, piece), bf16),
-        ]
-
-    def landing():
-        return [
-            pltpu.VMEM((PIECES, 256, piece), bf16), pltpu.VMEM((PIECES, 2, 256, piece), bf16),
-            pltpu.VMEM((PIECES, 3, 64, piece), bf16), pltpu.VMEM((32, half), f32), pltpu.VMEM((32, half), f32),
+            pltpu.VMEM((PIECES, 4, set_rows, half), bf16), pltpu.VMEM((PIECES, 4, set_rows, half), bf16),
+            pltpu.VMEM((PIECES, 4, set_rows, half), bf16), pltpu.VMEM((PIECES, set_rows, half), f32),
+            pltpu.VMEM((PIECES, set_rows, half), bf16), pltpu.VMEM((PIECES, 2, set_rows, half), bf16),
+            pltpu.VMEM((PIECES, 3, 2 * PART, half), bf16), pltpu.VMEM((PIECES, PART, half), f32),
+            pltpu.VMEM((PIECES, PART, half), f32),
         ]
 
     return pl.pallas_call(
@@ -390,8 +429,7 @@
             pltpu.VMEM(w_out.shape, bf16), pltpu.VMEM(w_gu.shape, bf16), pltpu.VMEM(w_down.shape, bf16),
             pltpu.SemaphoreType.DMA((3,)), pltpu.SemaphoreType.DMA((TAIL_ROLES,)),
             pltpu.SemaphoreType.DMA((TAIL_ROLES,)),
-            *travel(), pltpu.VMEM((PIECES, 256, piece), f32), *landing(),
-            *travel(), *landing(),
+            *scatter_scratch(), *scatter_scratch(),
             pltpu.VMEM((tok_grp, width), bf16), pltpu.VMEM((tok_grp, units), bf16),
         ],
         compiler_params=pltpu.CompilerParams(
@@ -512,33 +550,39 @@
     latent = jnp.dot(normed, w_latent[...], preferred_element_type=f32)
     rows_buf[own_rows, pl.ds(width, 128)] = latent.astype(bf16)
     gather = Gather(mail, 0, rows_buf, 32)
-    for stage in gather.stages():
-        if stage == "relay0":
-            y_pass(0)
-        if stage == "relay2":
-            y_pass(1)
-        if stage == "relay3":
-            deal(0)
-    deal(1)
-    gather.finish()
-
-    w_load.wait()
     contract = (((1,), (1,)), ((), ()))
-    pad = jnp.zeros((256, 256 - HD), bf16)
-
-    @pl.loop(0, 4)
-    def _(i):
-        at = pl.ds(pl.multiple_of(i * 256, 256), 256)
-        rows = rows_buf[at, pl.ds(0, width)]
+
+    def project(own, partners):
+        gather.from_partner(*partners)
+        places = [gather.owner(*at) for at in own] + [gather.owner(*at, True) for at in partners]
+        slices = [pl.ds(pl.multiple_of(place * 32, 32), 32) for place in places]
+        rows = jnp.concatenate([rows_buf[at, pl.ds(0, width)] for at in slices], axis=0)
+        latents = jnp.concatenate([rows_buf[at, pl.ds(width, 128)] for at in slices], axis=0)
+        pad = jnp.zeros((rows.shape[0], 256 - HD), bf16)
         for part in range(3):
             value = lax.dot_general(
                 rows, w_qkv[pl.ds(part * HD, HD), :], contract, preferred_element_type=f32
             )
             if part == 0:
-                value = value + lax.dot_general(
-                    rows_buf[at, pl.ds(width, 128)], up_ref[...], contract, preferred_element_type=f32
-                )
-            qkv[part, at, :] = jnp.concatenate([value.astype(bf16), pad], axis=1)
+                value = value + lax.dot_general(latents, up_ref[...], contract, preferred_element_type=f32)
+            value = jnp.concatenate([value.astype(bf16), pad], axis=1)
+            for n, at in enumerate(slices):
+                qkv[part, at, :] = value[n * 32:(n + 1) * 32]
+
+    for stage in gather.stages():
+        if stage == "relay0":
+            y_pass(0)
+        if stage == "relay2":
+            w_load.wait()
+            project([(0, 0), (0, 1), (0, 2), (1, 0), (2, 0)], [(0, 0), (0, 1), (0, 2)])
+        if stage == "relay3":
+            y_pass(1)
+            project([(1, 1), (2, 1), (1, 2), (2, 2), (0, 3), (3, 0)], [(1, 0), (2, 0)])
+            deal(0)
+        if stage == "far3":
+            project([(1, 3), (2, 3)], [(0, 3), (1, 1), (2, 1), (1, 2), (2, 2), (3, 0)])
+    deal(1)
+    project([(3, 1), (3, 2), (3, 3)], [(1, 3), (2, 3), (3, 1), (3, 2), (3, 3)])
 
     dealt(0)
 

time: 194 us -> 186 us (0.959)
  Pallas kernels: 193 us -> 184 us
    pallas_call x1, Pallas kernels: 89.4 us -> 83.4 us  [front(): pl.pallas_call(front_kernel, out_shape=jax.ShapeDtypeStruct((tok_grp, HD)...]
    pallas_call x1, Pallas kernels: 102 us -> 98.5 us  [tail(): pl.pallas_call(tail_kernel, out_shape=(jax.ShapeDtypeStruct((32, width),...]
where the time goes in v4:
time: 186 us; the launch traced here: 184 us
  Pallas kernels  184 us (99%)
    pallas_call x1, Pallas kernels, tail(): pl.pallas_call(tail_kernel, out_shape=(jax.ShapeDtypeStruct((32, width),...  98.5 us
    pallas_call x1, Pallas kernels, front(): pl.pallas_call(front_kernel, out_shape=jax.ShapeDtypeStruct((tok_grp, HD)...  83.4 us

profile of v4, /device:TPU:1, one launch (start us, length us, event | category | flops | bytes accessed | tf_op | source)
XLA Modules:
  0.0 184.4 jit_solution(6812749878460802201)
XLA Ops:
  0.6 83.4 %front.1.heads_ref = bf16[1024,224]{1,0:T(8,128)(2,1)} custom-call(s32[3]{0:T(128)} %slot_ref.1, s32[4]{0:T(128)} %choice_ref.1, s32[1,6]{1,0:T(1,128)} %lengths_ref.1, bf16[32,7168]{1,0:T(8,128)(2,1)} %tokens_ref.1, f32[7168]{0:T(1024)} %gain_ref.2, bf16[7168,128]{1,0:T(8,128)(2,1)} %down_hbm.1, bf16[224,128]{1,0:T(8,128)(2,1)} %bitcast.11, ...), custom_call_target="tpu_custom_call" | custom-call | tf_op jit(solution)/shard_map/front/pallas_call | solution.py:646
  84.1 98.5 %tail.1 = (bf16[32,3584]{1,0:T(8,128)(2,1)}, bf16[32,3584]{1,0:T(8,128)(2,1)}) custom-call(bf16[1024,224]{1,0:T(8,128)(2,1)} %front.1.heads_ref, bf16[224,3584]{1,0:T(8,128)(2,1)} %w_out_hbm.1, f32[3584]{0:T(1024)} %gain_ref.3, bf16[896,3584]{1,0:T(8,128)(2,1)} %bitcast.9, bf16[448,3584]{1,0:T(8,128)(2,1)} %w_down_hbm.1), custom_call_target="tpu_custom_call" | custom-call | tf_op jit(solution)/shard_map/tail/pallas_call | solution.py:423
  182.5 1.8 settle.1

commit v5 on v4

--- a/solution.py
+++ b/solution.py
@@ -350,31 +350,36 @@
     loads[0].wait()
     outer.far_sets(0)
     outer.next_sets(0)
+    outer.pass_on(0)
     outer.far_sets(1)
-    outer.pass_on(0)
     outer.next_sets(1)
     outer.own_set(0)
     outer.second(0)
     outer.pass_on(1)
     outer.own_set(1)
-    first = outer.settle(0)
+    stages = [gather.stages() for gather in gathers]
+    normalise(0, outer.settle(0))
+    next(stages[0])
     outer.second(1)
-    stages = [gather.stages() for gather in gathers]
-    normalise(0, first)
+    assert next(stages[0]) == "relay0"
+    normalise(1, outer.settle(1))
+    next(stages[1])
+    assert next(stages[0]) == "relay1"
+    assert next(stages[1]) == "relay0"
+    assert next(stages[0]) == "relay2"
+    assert next(stages[1]) == "relay1"
     next(stages[0])
-    second = outer.settle(1)
-    normalise(1, second)
+    assert next(stages[0]) == "relay3"
+    assert next(stages[1]) == "relay2"
     next(stages[1])
-    for name in ("relay0", "relay1", "relay2", "far0", "relay3"):
-        for stage in stages:
-            assert next(stage) == name
     for name in ("far1", "far2", "far3"):
-        next(stages[0])
+        assert next(stages[0]) == name
+    assert next(stages[1]) == "relay3"
     loads[1].wait()
     gathers[0].finish()
     feed(0, 0)
     for name in ("far1", "far2", "far3"):
-        next(stages[1])
+        assert next(stages[1]) == name
     feed(0, 1)
     loads[2].wait()
     inner.far_sets(0)
@@ -439,15 +444,15 @@
     )(heads_out, w_out, gain_ff, w_gu, w_down)
 
 
-FRONT_BLOCKS = 36
+CHUNKS = 4
+STEP = 8
 WINDOW = 768
 
 
 def front_kernel(
     slot_ref, choice_ref, lengths_ref, tokens_ref, gain_ref, down_hbm, up_ref, w_hbm, cache_hbm, heads_ref,
     w_qkv, w_latent, rows_buf, load_sems, send_sems, recv_sems,
-    first_0, first_1, second_0, second_1, pass_0, pass_1, split_0, split_1,
-    prefix, qkv, top, denom, total,
+    prefix, qkv, top, denom, total, *chunked,
 ):
     x, z, c = place()
     hid = lax.axis_index("hid")
@@ -455,8 +460,7 @@
     lower, upper = (req + 3) % 4, (req + 1) % 4
     width = tokens_ref.shape[1]
     bf16, f32 = jnp.bfloat16, jnp.float32
-    first, second = (first_0, first_1), (second_0, second_1)
-    passed, split = (pass_0, pass_1), (split_0, split_1)
+    first, second, passed, split = (chunked[n * CHUNKS:(n + 1) * CHUNKS] for n in range(4))
 
     def owner(group):
         return slot_ref[choice_ref[group]]
@@ -465,14 +469,15 @@
     barrier = pltpu.get_barrier_semaphore()
     for peer in peers:
         pl.semaphore_signal(barrier, inc=1, device_id=peer, device_id_type=MESH)
-    latent_load = pltpu.make_async_copy(down_hbm, w_latent, load_sems.at[5])
+    latent_load = pltpu.make_async_copy(down_hbm, w_latent, load_sems.at[1])
     latent_load.start()
+    def part_of(half, k):
+        return cache_hbm.at[pl.ds(half * STEP * CHUNKS + k * STEP, STEP)]
+
     loads = []
-    for k in range(2):
+    for k in range(CHUNKS):
         for half in range(2):
-            copy = pltpu.make_async_copy(
-                cache_hbm.at[pl.ds(half * 32 + k * 16, 16)], first[k].at[half], load_sems.at[1 + 2 * k + half]
-            )
+            copy = pltpu.make_async_copy(part_of(half, k), first[k].at[half], load_sems.at[2 + 2 * k + half])
             copy.start()
             loads.append(copy)
     w_load = pltpu.make_async_copy(w_hbm, w_qkv, load_sems.at[0])
@@ -486,7 +491,8 @@
 
     mail = Mail(send_sems, recv_sems)
     y_base = GATHER_ROLES
-    deal_base = y_base + 8
+    deal_base = y_base + 4 * CHUNKS
+    deal_rows = 2 * STEP
 
     def y_copy(role, src, dst, to):
         return pltpu.make_async_remote_copy(
@@ -500,23 +506,23 @@
         mail.sent[role] = copy
 
     def y_start():
-        for k in range(2):
-            y_send(y_base + k, cache_hbm.at[pl.ds(k * 16, 16)], first[k].at[2], lower)
-            y_send(y_base + 2 + k, cache_hbm.at[pl.ds(32 + k * 16, 16)], first[k].at[3], upper)
+        for k in range(CHUNKS):
+            y_send(y_base + k, part_of(0, k), first[k].at[2], lower)
+            y_send(y_base + CHUNKS + k, part_of(1, k), first[k].at[3], upper)
 
     def y_pass(k):
         loads[2 * k].wait()
         loads[2 * k + 1].wait()
         y_copy(y_base + k, first[k].at[2], first[k].at[2], upper).wait_recv()
-        y_copy(y_base + 2 + k, first[k].at[3], first[k].at[3], lower).wait_recv()
+        y_copy(y_base + CHUNKS + k, first[k].at[3], first[k].at[3], lower).wait_recv()
         passed[k][0] = first[k][jnp.where(owner(lower) == req, 1, 2)]
-        y_send(y_base + 4 + k, passed[k].at[0], second[k].at[0], lower)
+        y_send(y_base + 2 * CHUNKS + k, passed[k].at[0], second[k].at[0], lower)
         passed[k][1] = first[k][jnp.where(owner(upper) == req, 0, 3)]
-        y_send(y_base + 6 + k, passed[k].at[1], second[k].at[1], upper)
+        y_send(y_base + 3 * CHUNKS + k, passed[k].at[1], second[k].at[1], upper)
 
     def deal(k):
-        y_copy(y_base + 4 + k, second[k].at[0], second[k].at[0], upper).wait_recv()
-        y_copy(y_base + 6 + k, second[k].at[1], second[k].at[1], lower).wait_recv()
+        y_copy(y_base + 2 * CHUNKS + k, second[k].at[0], second[k].at[0], upper).wait_recv()
+        y_copy(y_base + 3 * CHUNKS + k, second[k].at[1], second[k].at[1], lower).wait_recv()
         away = (owner(req) - req + 4) % 4
         late_a = jnp.full((1, 1, 1), (away >= 2).astype(jnp.int32)) > 0
         late_b = jnp.full((1, 1, 1), jnp.logical_or(away == 1, away == 2).astype(jnp.int32)) > 0
@@ -525,25 +531,27 @@
         r = lax.broadcasted_iota(jnp.int32, (32, 32), 0)
         s = lax.broadcasted_iota(jnp.int32, (32, 32), 1)
         sort = (s == jnp.where(r < 16, 2 * r, 2 * r - 31)).astype(bf16)
-        zeros = jnp.zeros((16, 256 - HD), bf16)
-        for half, value in enumerate((half_a, half_b)):
-            planes = jnp.dot(sort, value.reshape(32, width), preferred_element_type=f32).astype(bf16)
-            for kv in range(2):
-                for h in range(32):
-                    piece = planes[kv * 16:(kv + 1) * 16, h * HD:(h + 1) * HD]
-                    split[k][h, kv, pl.ds(half * 16, 16), :] = jnp.concatenate([piece, zeros], axis=1)
-
-        landing = prefix.at[k, :, own_rows]
+        zeros = jnp.zeros((deal_rows, 256 - HD), bf16)
+        value = jnp.concatenate([half_a.reshape(2 * STEP, width), half_b.reshape(2 * STEP, width)], axis=0)
+        planes = jnp.dot(sort, value, preferred_element_type=f32).astype(bf16)
+        for kv in range(2):
+            for h in range(32):
+                piece = planes[kv * deal_rows:(kv + 1) * deal_rows, h * HD:(h + 1) * HD]
+                split[k][h, kv] = jnp.concatenate([piece, zeros], axis=1)
+
         for d in range(1, 32):
             to = (hid + d) % 32
-            mail.send(deal_base + k * 31 + d - 1, split[k].at[to], landing, to)
-        prefix[k, :, own_rows] = split[k][hid]
+            mail.send(deal_base + k * 31 + d - 1, split[k].at[to], landing(k, hid), to)
+        prefix[:, pl.ds(pl.multiple_of(k * 512 + hid * deal_rows, deal_rows), deal_rows)] = split[k][hid]
+
+    def landing(k, source):
+        start = pl.multiple_of(k * 512 + source * deal_rows, deal_rows)
+        return prefix.at[:, pl.ds(start, deal_rows)]
 
     def dealt(k):
         for d in range(1, 32):
             source = (hid + 32 - d) % 32
-            landing = prefix.at[k, :, pl.ds(pl.multiple_of(source * 32, 32), 32)]
-            mail.await_recv(deal_base + k * 31 + d - 1, landing, source)
+            mail.await_recv(deal_base + k * 31 + d - 1, landing(k, source), source)
 
     y_start()
     latent_load.wait()
@@ -572,19 +580,25 @@
     for stage in gather.stages():
         if stage == "relay0":
             y_pass(0)
+            y_pass(1)
         if stage == "relay2":
             w_load.wait()
             project([(0, 0), (0, 1), (0, 2), (1, 0), (2, 0)], [(0, 0), (0, 1), (0, 2)])
+            y_pass(2)
+            y_pass(3)
         if stage == "relay3":
-            y_pass(1)
             project([(1, 1), (2, 1), (1, 2), (2, 2), (0, 3), (3, 0)], [(1, 0), (2, 0)])
             deal(0)
+        if stage == "far1":
+            deal(1)
         if stage == "far3":
+            deal(2)
             project([(1, 3), (2, 3)], [(0, 3), (1, 1), (2, 1), (1, 2), (2, 2), (3, 0)])
-    deal(1)
+    deal(3)
     project([(3, 1), (3, 2), (3, 3)], [(1, 3), (2, 3), (3, 1), (3, 2), (3, 3)])
 
     dealt(0)
+    dealt(1)
 
     ends = [lengths_ref[0, 0]]
     for n in range(1, lengths_ref.shape[1]):
@@ -597,7 +611,7 @@
         begin = jnp.minimum(jnp.maximum(i * 128 - 512, 0), 1024 - WINDOW)
         near = pl.ds(pl.multiple_of(begin, 128), WINDOW)
         q = qkv[0, at, :]
-        s_far = lax.dot_general(q, prefix[0, 0], contract, preferred_element_type=f32) * factor
+        s_far = lax.dot_general(q, prefix[0, pl.ds(0, 1024), :], contract, preferred_element_type=f32) * factor
         s_near = lax.dot_general(q, qkv[1, near, :], contract, preferred_element_type=f32) * factor
         row = lax.broadcasted_iota(jnp.int32, (128, 1), 0) + i * 128
         since = jnp.zeros((128, 1), jnp.int32)
@@ -612,21 +626,32 @@
         e_near = jnp.exp(s_near - row_max)
         top[at, :] = row_max
         denom[at, :] = jnp.sum(e_far, axis=1, keepdims=True) + jnp.sum(e_near, axis=1, keepdims=True)
-        out = jnp.dot(e_far.astype(bf16), prefix[0, 1], preferred_element_type=f32)
+        out = jnp.dot(e_far.astype(bf16), prefix[1, pl.ds(0, 1024), :], preferred_element_type=f32)
         total[at, :] = out + jnp.dot(e_near.astype(bf16), qkv[2, near, :], preferred_element_type=f32)
 
-    dealt(1)
-
-    @pl.loop(0, 8)
-    def _(i):
-        at = pl.ds(pl.multiple_of(i * 128, 128), 128)
-        scores = lax.dot_general(qkv[0, at, :], prefix[1, 0], contract, preferred_element_type=f32) * factor
-        row_max = jnp.maximum(top[at, :], jnp.max(scores, axis=1, keepdims=True))
-        keep = jnp.exp(top[at, :] - row_max)
-        expos = jnp.exp(scores - row_max)
-        row_sum = denom[at, :] * keep + jnp.sum(expos, axis=1, keepdims=True)
-        out = total[at, :] * keep + jnp.dot(expos.astype(bf16), prefix[1, 1], preferred_element_type=f32)
-        heads_ref[at, :] = (out / row_sum)[:, :HD].astype(bf16)
+    for k in (2, 3):
+        dealt(k)
+        more = pl.ds(k * 512, 512)
+
+        @pl.loop(0, 4)
+        def _(i):
+            at = pl.ds(pl.multiple_of(i * 256, 256), 256)
+            scores = lax.dot_general(
+                qkv[0, at, :], prefix[0, more, :], contract, preferred_element_type=f32
+            ) * factor
+            row_max = jnp.maximum(top[at, :], jnp.max(scores, axis=1, keepdims=True))
+            keep = jnp.exp(top[at, :] - row_max)
+            expos = jnp.exp(scores - row_max)
+            row_sum = denom[at, :] * keep + jnp.sum(expos, axis=1, keepdims=True)
+            out = total[at, :] * keep + jnp.dot(
+                expos.astype(bf16), prefix[1, more, :], preferred_element_type=f32
+            )
+            if k == 2:
+                top[at, :] = row_max
+                denom[at, :] = row_sum
+                total[at, :] = out
+            else:
+                heads_ref[at, :] = (out / row_sum)[:, :HD].astype(bf16)
 
     mail.drain()
 
@@ -638,10 +663,10 @@
     smem = pl.BlockSpec(memory_space=pltpu.SMEM)
     vmem = pl.BlockSpec(memory_space=pltpu.VMEM)
     anywhere = pl.BlockSpec(memory_space=pl.ANY)
-    roles = GATHER_ROLES + 8 + 62
+    roles = GATHER_ROLES + 4 * CHUNKS + 31 * CHUNKS
 
     def halves(count):
-        return pltpu.VMEM((count, 16, 2, width), bf16)
+        return [pltpu.VMEM((count, STEP, 2, width), bf16)] * CHUNKS
 
     return pl.pallas_call(
         front_kernel,
@@ -651,13 +676,13 @@
         scratch_shapes=[
             pltpu.VMEM(w_t.shape, bf16), pltpu.VMEM(adapt_down.shape, bf16),
             pltpu.VMEM((tok_grp, width + 128), bf16),
-            pltpu.SemaphoreType.DMA((6,)), pltpu.SemaphoreType.DMA((roles,)),
+            pltpu.SemaphoreType.DMA((2 + 2 * CHUNKS,)), pltpu.SemaphoreType.DMA((roles,)),
             pltpu.SemaphoreType.DMA((roles,)),
-            halves(4), halves(4), halves(2), halves(2), halves(2), halves(2),
-            pltpu.VMEM((32, 2, 32, 256), bf16), pltpu.VMEM((32, 2, 32, 256), bf16),
-            pltpu.VMEM((2, 2, tok_grp, 256), bf16), pltpu.VMEM((3, tok_grp, 256), bf16),
+            pltpu.VMEM((2, 2048, 256), bf16), pltpu.VMEM((3, tok_grp, 256), bf16),
             pltpu.VMEM((tok_grp, 1), jnp.float32), pltpu.VMEM((tok_grp, 1), jnp.float32),
             pltpu.VMEM((tok_grp, 256), jnp.float32),
+            *halves(4), *halves(2), *halves(2),
+            *([pltpu.VMEM((32, 2, 2 * STEP, 256), bf16)] * CHUNKS),
         ],
         compiler_params=pltpu.CompilerParams(
             collective_id=1, has_side_effects=True, vmem_limit_bytes=66000000

time: 186 us -> 183 us (0.984)
  Pallas kernels: 184 us -> 182 us
where the time goes in v5:
time: 183 us
  Pallas kernels  182 us (99%)
    pallas_call x1, Pallas kernels, tail(): pl.pallas_call(tail_kernel, out_shape=(jax.ShapeDtypeStruct((32, width),...  97 us
    pallas_call x1, Pallas kernels, front(): pl.pallas_call(front_kernel, out_shape=jax.ShapeDtypeStruct((tok_grp, HD)...  83.4 us

profile of v5, /device:TPU:1, one launch (start us, length us, event | category | flops | bytes accessed | tf_op | source)
XLA Modules:
  0.0 182.8 jit_solution(12055380115271924148)
XLA Ops:
  0.6 83.4 %front.1.heads_ref = bf16[1024,224]{1,0:T(8,128)(2,1)} custom-call(s32[3]{0:T(128)} %slot_ref.1, s32[4]{0:T(128)} %choice_ref.1, s32[1,6]{1,0:T(1,128)} %lengths_ref.1, bf16[32,7168]{1,0:T(8,128)(2,1)} %tokens_ref.1, f32[7168]{0:T(1024)} %gain_ref.2, bf16[7168,128]{1,0:T(8,128)(2,1)} %down_hbm.1, bf16[224,128]{1,0:T(8,128)(2,1)} %bitcast.11, ...), custom_call_target="tpu_custom_call" | custom-call | tf_op jit(solution)/shard_map/front/pallas_call | solution.py:671
  84.0 97.0 %tail.1 = (bf16[32,3584]{1,0:T(8,128)(2,1)}, bf16[32,3584]{1,0:T(8,128)(2,1)}) custom-call(bf16[1024,224]{1,0:T(8,128)(2,1)} %front.1.heads_ref, bf16[224,3584]{1,0:T(8,128)(2,1)} %w_out_hbm.1, f32[3584]{0:T(1024)} %gain_ref.3, bf16[896,3584]{1,0:T(8,128)(2,1)} %bitcast.9, bf16[448,3584]{1,0:T(8,128)(2,1)} %w_down_hbm.1), custom_call_target="tpu_custom_call" | custom-call | tf_op jit(solution)/shard_map/tail/pallas_call | solution.py:428
  181.0 1.8 %settle.1 = (bf16[32,3584]{1,0:T(8,128)(2,1)}, bf16[32,3584]{1,0:T(8,128)(2,1)}) custom-call(bf16[32,3584]{1,0:T(8,128)(2,1)} %get-tuple-element.4.attn_ref, bf16[32,3584]{1,0:T(8,128)(2,1)} %get-tuple-element.5.block_ref), custom_call_target="tpu_custom_call" | custom-call | tf_op jit(solution)/shard_map/settle/pallas_call | solution.py:701

commit v6 on v5

--- a/solution.py
+++ b/solution.py
@@ -173,6 +173,7 @@
         self.xs, self.xr, self.sums, self.acc = xs, xr, sums, acc
         self.near, self.mid, self.last = near, mid, last
         self.swap_out, self.swap_in = swap_out, swap_in
+        self.made = set()
         x, z, c = place()
         self.c = c
         self.a = (1 - c) * z + c * x
@@ -188,10 +189,15 @@
     def set_chips(self, k, cc):
         return [(1 - cc) * (j * 4 + k) + cc * (k * 4 + j) for j in range(4)]
 
+    def partner_product(self, p, idx):
+        c, step = self.c, (2, 1, 3, 0)[idx]
+        if (p, idx) not in self.made:
+            self.made.add((p, idx))
+            chips = self.set_chips((self.b + step) % 4, 1 - c)
+            self.product(chips, 1 - c, p, self.xs.at[p, idx], None)
+
     def partner_part(self, p, idx):
-        c, step = self.c, (2, 1, 3, 0)[idx]
-        chips = self.set_chips((self.b + step) % 4, 1 - c)
-        self.product(chips, 1 - c, p, self.xs.at[p, idx], None)
+        self.partner_product(p, idx)
         self.mail.send(self.role(p, idx), self.xs.at[p, idx], self.xr.at[p, idx], self.partner)
 
     def own_part(self, p, idx, out):
@@ -287,7 +293,6 @@
         pl.semaphore_signal(barrier, inc=1, device_id=peer, device_id_type=MESH)
     for load in loads:
         load.start()
-    pl.semaphore_wait(barrier, len(peers))
     mail = Mail(send_sems, recv_sems)
     width = w_out.shape[1] // 2
     units = w_down.shape[0]
@@ -348,6 +353,9 @@
         hidden[at, :] = (jax.nn.silu(gate) * up).astype(jnp.bfloat16)
 
     loads[0].wait()
+    outer.partner_product(0, 0)
+    outer.partner_product(0, 1)
+    pl.semaphore_wait(barrier, len(peers))
     outer.far_sets(0)
     outer.next_sets(0)
     outer.pass_on(0)
@@ -446,12 +454,25 @@
 
 CHUNKS = 4
 STEP = 8
+
+
+def deal_order():
+    near = [(0, dz, dc) for dc in range(2) for dz in (1, 3, 2)] + [(0, 0, 1)]
+    order = []
+    for n in range(8):
+        order += [(dx, n % 4, n // 4) for dx in (1, 3, 2)] + near[n:n + 1]
+    return order
+
+
+def at_offset(dx, dz, dc, sign=1):
+    x, z, c = place()
+    return ((x + 4 + sign * dx) % 4) * 8 + ((z + 4 + sign * dz) % 4) * 2 + (c + dc) % 2
 WINDOW = 768
 
 
 def front_kernel(
     slot_ref, choice_ref, lengths_ref, tokens_ref, gain_ref, down_hbm, up_ref, w_hbm, cache_hbm, heads_ref,
-    w_qkv, w_latent, rows_buf, load_sems, send_sems, recv_sems,
+    w_qkv, w_latent, rows_buf, latents_buf, load_sems, send_sems, recv_sems,
     prefix, qkv, top, denom, total, *chunked,
 ):
     x, z, c = place()
@@ -486,7 +507,7 @@
     matrix = tokens_ref[...].astype(f32)
     normed = rms_scale(matrix, gain_ref[...].reshape(1, width)).astype(bf16)
     own_rows = pl.ds(pl.multiple_of(hid * 32, 32), 32)
-    rows_buf[own_rows, pl.ds(0, width)] = normed
+    rows_buf[own_rows, :] = normed
     pl.semaphore_wait(barrier, len(peers))
 
     mail = Mail(send_sems, recv_sems)
@@ -539,9 +560,9 @@
                 piece = planes[kv * deal_rows:(kv + 1) * deal_rows, h * HD:(h + 1) * HD]
                 split[k][h, kv] = jnp.concatenate([piece, zeros], axis=1)
 
-        for d in range(1, 32):
-            to = (hid + d) % 32
-            mail.send(deal_base + k * 31 + d - 1, split[k].at[to], landing(k, hid), to)
+        for n, offset in enumerate(deal_order()):
+            to = at_offset(*offset)
+            mail.send(deal_base + k * 31 + n, split[k].at[to], landing(k, hid), to)
         prefix[:, pl.ds(pl.multiple_of(k * 512 + hid * deal_rows, deal_rows), deal_rows)] = split[k][hid]
 
     def landing(k, source):
@@ -549,40 +570,61 @@
         return prefix.at[:, pl.ds(start, deal_rows)]
 
     def dealt(k):
-        for d in range(1, 32):
-            source = (hid + 32 - d) % 32
-            mail.await_recv(deal_base + k * 31 + d - 1, landing(k, source), source)
+        for n, offset in enumerate(deal_order()):
+            source = at_offset(*offset, sign=-1)
+            mail.await_recv(deal_base + k * 31 + n, landing(k, source), source)
 
     y_start()
-    latent_load.wait()
-    latent = jnp.dot(normed, w_latent[...], preferred_element_type=f32)
-    rows_buf[own_rows, pl.ds(width, 128)] = latent.astype(bf16)
     gather = Gather(mail, 0, rows_buf, 32)
+    latent_base = deal_base + 31 * CHUNKS
+
+    def latent_rows(device):
+        return latents_buf.at[pl.ds(pl.multiple_of(device * 32, 32), 32)]
+
+    def send_latents():
+        latent_load.wait()
+        latent = jnp.dot(normed, w_latent[...], preferred_element_type=f32)
+        latents_buf[own_rows, :] = latent.astype(bf16)
+        for n, offset in enumerate(deal_order()):
+            mail.send(latent_base + n, latent_rows(hid), latent_rows(hid), at_offset(*offset))
+
+    def await_latents():
+        for n, offset in enumerate(deal_order()):
+            source = at_offset(*offset, sign=-1)
+            mail.await_recv(latent_base + n, latent_rows(source), source)
+
     contract = (((1,), (1,)), ((), ()))
 
     def project(own, partners):
         gather.from_partner(*partners)
         places = [gather.owner(*at) for at in own] + [gather.owner(*at, True) for at in partners]
         slices = [pl.ds(pl.multiple_of(place * 32, 32), 32) for place in places]
-        rows = jnp.concatenate([rows_buf[at, pl.ds(0, width)] for at in slices], axis=0)
-        latents = jnp.concatenate([rows_buf[at, pl.ds(width, 128)] for at in slices], axis=0)
+        rows = jnp.concatenate([rows_buf[at, :] for at in slices], axis=0)
+        latents = jnp.concatenate([latents_buf[at, :] for at in slices], axis=0)
         pad = jnp.zeros((rows.shape[0], 256 - HD), bf16)
-        for part in range(3):
-            value = lax.dot_general(
-                rows, w_qkv[pl.ds(part * HD, HD), :], contract, preferred_element_type=f32
-            )
-            if part == 0:
-                value = value + lax.dot_general(latents, up_ref[...], contract, preferred_element_type=f32)
+
+        def keep(part, value):
             value = jnp.concatenate([value.astype(bf16), pad], axis=1)
             for n, at in enumerate(slices):
                 qkv[part, at, :] = value[n * 32:(n + 1) * 32]
 
+        value = lax.dot_general(rows, w_qkv[pl.ds(0, HD), :], contract, preferred_element_type=f32)
+        keep(0, value + lax.dot_general(latents, up_ref[...], contract, preferred_element_type=f32))
+
+        @pl.loop(1, 3)
+        def _(part):
+            weight = w_qkv[pl.ds(pl.multiple_of(part * HD, 32), HD), :]
+            keep(part, lax.dot_general(rows, weight, contract, preferred_element_type=f32))
+
     for stage in gather.stages():
+        if stage == "start":
+            send_latents()
         if stage == "relay0":
             y_pass(0)
             y_pass(1)
         if stage == "relay2":
             w_load.wait()
+            await_latents()
             project([(0, 0), (0, 1), (0, 2), (1, 0), (2, 0)], [(0, 0), (0, 1), (0, 2)])
             y_pass(2)
             y_pass(3)
@@ -593,8 +635,8 @@
             deal(1)
         if stage == "far3":
             deal(2)
+            deal(3)
             project([(1, 3), (2, 3)], [(0, 3), (1, 1), (2, 1), (1, 2), (2, 2), (3, 0)])
-    deal(3)
     project([(3, 1), (3, 2), (3, 3)], [(1, 3), (2, 3), (3, 1), (3, 2), (3, 3)])
 
     dealt(0)
@@ -663,7 +705,7 @@
     smem = pl.BlockSpec(memory_space=pltpu.SMEM)
     vmem = pl.BlockSpec(memory_space=pltpu.VMEM)
     anywhere = pl.BlockSpec(memory_space=pl.ANY)
-    roles = GATHER_ROLES + 4 * CHUNKS + 31 * CHUNKS
+    roles = GATHER_ROLES + 4 * CHUNKS + 31 * (CHUNKS + 1)
 
     def halves(count):
         return [pltpu.VMEM((count, STEP, 2, width), bf16)] * CHUNKS
@@ -675,7 +717,7 @@
         out_specs=vmem,
         scratch_shapes=[
             pltpu.VMEM(w_t.shape, bf16), pltpu.VMEM(adapt_down.shape, bf16),
-            pltpu.VMEM((tok_grp, width + 128), bf16),
+            pltpu.VMEM((tok_grp, width), bf16), pltpu.VMEM((tok_grp, 128), bf16),
             pltpu.SemaphoreType.DMA((2 + 2 * CHUNKS,)), pltpu.SemaphoreType.DMA((roles,)),
             pltpu.SemaphoreType.DMA((roles,)),
             pltpu.VMEM((2, 2048, 256), bf16), pltpu.VMEM((3, tok_grp, 256), bf16),

time: 183 us -> 178 us (0.973)
  Pallas kernels: 182 us -> 178 us
    pallas_call x1, Pallas kernels: 97 us -> 90.1 us  [tail(): pl.pallas_call(tail_kernel, out_shape=(jax.ShapeDtypeStruct((32, width),...]
    pallas_call x1, Pallas kernels: 83.4 us -> 85.6 us  [front(): pl.pallas_call(front_kernel, out_shape=jax.ShapeDtypeStruct((tok_grp, HD)...]
where the time goes in v6:
time: 178 us
  Pallas kernels  178 us (100%)
    pallas_call x1, Pallas kernels, tail(): pl.pallas_call(tail_kernel, out_shape=(jax.ShapeDtypeStruct((32, width),...  90.1 us
    pallas_call x1, Pallas kernels, front(): pl.pallas_call(front_kernel, out_shape=jax.ShapeDtypeStruct((tok_grp, HD)...  85.6 us

profile of v6, /device:TPU:1, one launch (start us, length us, event | category | flops | bytes accessed | tf_op | source)
XLA Modules:
  0.0 178.2 jit_solution(3772966145401978005)
XLA Ops:
  0.6 85.6 %front.1.heads_ref = bf16[1024,224]{1,0:T(8,128)(2,1)} custom-call(s32[3]{0:T(128)} %slot_ref.1, s32[4]{0:T(128)} %choice_ref.1, s32[1,6]{1,0:T(1,128)} %lengths_ref.1, bf16[32,7168]{1,0:T(8,128)(2,1)} %tokens_ref.1, f32[7168]{0:T(1024)} %gain_ref.2, bf16[7168,128]{1,0:T(8,128)(2,1)} %down_hbm.1, bf16[224,128]{1,0:T(8,128)(2,1)} %bitcast.11, ...), custom_call_target="tpu_custom_call" | custom-call | tf_op jit(solution)/shard_map/front/pallas_call | solution.py:713
  86.3 90.1 %tail.1 = (bf16[32,3584]{1,0:T(8,128)(2,1)}, bf16[32,3584]{1,0:T(8,128)(2,1)}) custom-call(bf16[1024,224]{1,0:T(8,128)(2,1)} %front.1.heads_ref, bf16[224,3584]{1,0:T(8,128)(2,1)} %w_out_hbm.1, f32[3584]{0:T(1024)} %gain_ref.3, bf16[896,3584]{1,0:T(8,128)(2,1)} %bitcast.9, bf16[448,3584]{1,0:T(8,128)(2,1)} %w_down_hbm.1), custom_call_target="tpu_custom_call" | custom-call | tf_op jit(solution)/shard_map/tail/pallas_call | solution.py:436
  176.4 1.8 %settle.1 = (bf16[32,3584]{1,0:T(8,128)(2,1)}, bf16[32,3584]{1,0:T(8,128)(2,1)}) custom-call(bf16[32,3584]{1,0:T(8,128)(2,1)} %get-tuple-element.4.attn_ref, bf16[32,3584]{1,0:T(8,128)(2,1)} %get-tuple-element.5.block_ref), custom_call_target="tpu_custom_call" | custom-call | tf_op jit(solution)/shard_map/settle/pallas_call | solution.py:743

commit v7 on v6

--- a/solution.py
+++ b/solution.py
@@ -526,8 +526,8 @@
         copy.start()
         mail.sent[role] = copy
 
-    def y_start():
-        for k in range(CHUNKS):
+    def y_start(*chunks):
+        for k in chunks:
             y_send(y_base + k, part_of(0, k), first[k].at[2], lower)
             y_send(y_base + CHUNKS + k, part_of(1, k), first[k].at[3], upper)
 
@@ -574,7 +574,7 @@
             source = at_offset(*offset, sign=-1)
             mail.await_recv(deal_base + k * 31 + n, landing(k, source), source)
 
-    y_start()
+    y_start(0, 1)
     gather = Gather(mail, 0, rows_buf, 32)
     latent_base = deal_base + 31 * CHUNKS
 
@@ -619,24 +619,27 @@
     for stage in gather.stages():
         if stage == "start":
             send_latents()
+            y_pass(0)
+            y_start(2)
         if stage == "relay0":
-            y_pass(0)
             y_pass(1)
+            y_start(3)
         if stage == "relay2":
+            deal(0)
             w_load.wait()
             await_latents()
             project([(0, 0), (0, 1), (0, 2), (1, 0), (2, 0)], [(0, 0), (0, 1), (0, 2)])
             y_pass(2)
+        if stage == "relay3":
+            deal(1)
             y_pass(3)
-        if stage == "relay3":
             project([(1, 1), (2, 1), (1, 2), (2, 2), (0, 3), (3, 0)], [(1, 0), (2, 0)])
-            deal(0)
         if stage == "far1":
-            deal(1)
+            project([(1, 3), (2, 3)], [(0, 3), (1, 1), (2, 1), (1, 2), (2, 2), (3, 0)])
+        if stage == "far2":
+            deal(2)
         if stage == "far3":
-            deal(2)
             deal(3)
-            project([(1, 3), (2, 3)], [(0, 3), (1, 1), (2, 1), (1, 2), (2, 2), (3, 0)])
     project([(3, 1), (3, 2), (3, 3)], [(1, 3), (2, 3), (3, 1), (3, 2), (3, 3)])
 
     dealt(0)

time: 178 us -> 178 us (level)
  no operation moved by 1% of the time
where the time goes in v7:
time: 178 us
  Pallas kernels  177 us (99%)
    pallas_call x1, Pallas kernels, tail(): pl.pallas_call(tail_kernel, out_shape=(jax.ShapeDtypeStruct((32, width),...  89.5 us
    pallas_call x1, Pallas kernels, front(): pl.pallas_call(front_kernel, out_shape=jax.ShapeDtypeStruct((tok_grp, HD)...  85.8 us

profile of v7, /device:TPU:1, one launch (start us, length us, event | category | flops | bytes accessed | tf_op | source)
XLA Modules:
  0.0 177.9 jit_solution(12031511022376732362)
XLA Ops:
  0.6 85.8 %front.1.heads_ref = bf16[1024,224]{1,0:T(8,128)(2,1)} custom-call(s32[3]{0:T(128)} %slot_ref.1, s32[4]{0:T(128)} %choice_ref.1, s32[1,6]{1,0:T(1,128)} %lengths_ref.1, bf16[32,7168]{1,0:T(8,128)(2,1)} %tokens_ref.1, f32[7168]{0:T(1024)} %gain_ref.2, bf16[7168,128]{1,0:T(8,128)(2,1)} %down_hbm.1, bf16[224,128]{1,0:T(8,128)(2,1)} %bitcast.11, ...), custom_call_target="tpu_custom_call" | custom-call | tf_op jit(solution)/shard_map/front/pallas_call | solution.py:716
  86.5 89.5 %tail.1 = (bf16[32,3584]{1,0:T(8,128)(2,1)}, bf16[32,3584]{1,0:T(8,128)(2,1)}) custom-call(bf16[1024,224]{1,0:T(8,128)(2,1)} %front.1.heads_ref, bf16[224,3584]{1,0:T(8,128)(2,1)} %w_out_hbm.1, f32[3584]{0:T(1024)} %gain_ref.3, bf16[896,3584]{1,0:T(8,128)(2,1)} %bitcast.9, bf16[448,3584]{1,0:T(8,128)(2,1)} %w_down_hbm.1), custom_call_target="tpu_custom_call" | custom-call | tf_op jit(solution)/shard_map/tail/pallas_call | solution.py:436
  176.0 1.8 %settle.1 = (bf16[32,3584]{1,0:T(8,128)(2,1)}, bf16[32,3584]{1,0:T(8,128)(2,1)}) custom-call(bf16[32,3584]{1,0:T(8,128)(2,1)} %get-tuple-element.4.attn_ref, bf16[32,3584]{1,0:T(8,128)(2,1)} %get-tuple-element.5.block_ref), custom_call_target="tpu_custom_call" | custom-call | tf_op jit(solution)/shard_map/settle/pallas_call | solution.py:746
